TPU v7x, 32 devices: a whole 2x2x4 slice. The times are simulated.
32 devices in a mesh: section: 4 (over y, x), seq: 8 (over z, core).
Axes of the slice: x: 2, y: 2, z: 4, core: 2. Of those that a mesh axis runs over, the one named last changes fastest.
Arguments:
- tokens: bfloat16 [4096, 2048], P('seq', 'section'), may hold values from -6 to 6
- norm_gain: float32 [2048], replicated, may hold values from 0.25 to 1.75
- w_query: bfloat16 [2048, 2048], P('seq', 'section'), may hold values from -0.3125 to 0.3125
- w_key: bfloat16 [2048, 512], P('seq', 'section'), may hold values from -0.125 to 0.125
- w_value: bfloat16 [2048, 512], P('seq', 'section'), may hold values from -0.125 to 0.125
- w_out: bfloat16 [2048, 2048], P('seq', 'section'), may hold values from -0.25 to 0.25
- router_gate: float32 [4096], P('seq'), may hold values from 0.25 to 1
- chosen_blocks: int32 [8, 1], replicated, may hold values from 0 to 3, as said below
- block_counts: int32 [8], replicated, may hold values from 0 to 1, as said below
Outputs:
- mixed: bfloat16 [4096, 2048], P('seq', 'section')
Inputs may be any that keep to these rules, and one draw needn't show every extreme that they name: `chosen_blocks`: in each segment's row the entries name distinct blocks of 128 rows of that segment, in increasing order; only the first block_counts entries are used. `block_counts`: some segment has one chosen block and some segment has none.
All inputs are finite; a program needn't handle non-finite values.
Results may differ from a plain program's by a relative error of at most 0.0034.
Values may be sent and summed in bfloat16 or wider, within the bound.
A program may use at most 64 MiB of HBM per device.

v0:
```python
import functools
import math

import jax
import jax.numpy as jnp
from jax import lax
from jax.experimental import pallas as pl
from jax.experimental.pallas import tpu as pltpu
from jax.sharding import PartitionSpec as P

HEADS = 16
KV_HEADS = 4
HEAD_DIM = 128
BLOCK = 128
EPSILON = 1e-05
MESH = pl.DeviceIdType.MESH

KEY, VALUE, QUERY_A, QUERY_B, OUT_A, OUT_B, PANEL, GUEST_PANEL = range(8)


def repeat(low, high, body):
    if high - low <= 4:
        for step in range(low, high):
            body(step)
    elif high > low:

        def wrapped(step, carry):
            body(step)
            return carry

        lax.fori_loop(low, high, wrapped, 0)


def kernel(
    seq_count,
    section_count,
    tokens_ref,
    gain_ref,
    gate_ref,
    chosen_ref,
    count_ref,
    wq_in,
    wk_in,
    wv_in,
    wo_in,
    out_ref,
    rows_all,
    gate_rows,
    normed_ref,
    wk,
    wv,
    wq,
    wo,
    panel,
    queries_ref,
    numer_ref,
    denom_ref,
    heads_all,
    results,
    returned,
    recv,
    send_line,
    send_pair,
    own_sem,
    rows_send,
    rows_recv,
    heads_send,
    heads_recv,
    guest_send,
    guest_recv,
    back_send,
    back_recv,
    key_slots,
):
    me = lax.axis_index("seq")
    section = lax.axis_index("section")
    line = seq_count // 2
    spot = me // 2
    core = lax.rem(me, 2)
    pair = spot * 2 + 1 - core
    slots = chosen_ref.shape[0] // seq_count
    capacity, width = out_ref.shape
    kv_cols = wk_in.shape[1]
    groups = kv_cols // HEAD_DIM
    ratio = HEADS // KV_HEADS
    half_q = wq_in.shape[1] // 2
    half_o = wo_in.shape[1] // 2
    depth = section_count * width
    first, last = 1, line - 2
    active = (spot >= first) & (spot <= last)
    has_guest = (spot == first) | (spot == last)
    near = jnp.where(spot * 2 < line, 1, -1)
    guest_spot = spot - near
    guest = me - 2 * near
    host = me + 2 * near

    def rows_of(block, size):
        return pl.ds(pl.multiple_of(block * size, size), size)

    def full(chunk, block):
        if chunk == KEY:
            return wk.at[rows_of(block, wk_in.shape[0]), :]
        if chunk == VALUE:
            return wv.at[rows_of(block, wv_in.shape[0]), :]
        if chunk in (QUERY_A, QUERY_B):
            return wq.at[chunk - QUERY_A, rows_of(block, wq_in.shape[0]), :]
        if chunk in (PANEL, GUEST_PANEL):
            return panel.at[rows_of(block, capacity), :]
        return wo.at[chunk - OUT_A, rows_of(block, wo_in.shape[0]), :]

    def own(chunk):
        if chunk == KEY:
            return wk_in
        if chunk == VALUE:
            return wv_in
        if chunk in (QUERY_A, QUERY_B):
            return wq_in.at[:, pl.ds((chunk - QUERY_A) * half_q, half_q)]
        return wo_in.at[:, pl.ds((chunk - OUT_A) * half_o, half_o)]

    def transfer(chunk, block, send_sem, target, mine):
        return pltpu.make_async_remote_copy(
            src_ref=own(chunk) if mine else full(chunk, block),
            dst_ref=full(chunk, block),
            send_sem=send_sem,
            recv_sem=recv.at[min(chunk, PANEL), block],
            device_id={"seq": target},
            device_id_type=MESH,
        )

    def along(chunk, source, sign, mine):
        way = (1 - sign) // 2
        return transfer(
            chunk, source * 2 + core, send_line.at[way, min(chunk, PANEL), source], me + 2 * sign, mine
        )

    def across(chunk, source, mine):
        return transfer(
            chunk, source * 2 + core, send_pair.at[min(chunk, PANEL), source], pair, mine
        )

    def onward(sign):
        return (spot + sign >= first) & (spot + sign <= last)

    def begin(chunk, source):
        mine = chunk < PANEL
        for sign in (1, -1):

            @pl.when(onward(sign))
            def _():
                along(chunk, source, sign, mine).start()

        @pl.when(active)
        def _():
            across(chunk, source, mine).start()

    def relay(chunk, step, sign):
        source = spot - sign * step
        low, high = (first, last) if chunk >= PANEL else (0, line - 1)
        valid = active & (source >= low) & (source <= high)
        if chunk == GUEST_PANEL:
            valid = active & (source == jnp.where(sign > 0, first, last))
            source = source - sign

        @pl.when(valid)
        def _():
            across(chunk, source, False).wait_recv()

            @pl.when(onward(sign))
            def _():
                along(chunk, source, sign, False).start()

            across(chunk, source, False).start()

    def relay_all(chunks, low, high, sides=(1, -1)):
        def body(step):
            for side in sides:
                for chunk in chunks:
                    relay(chunk, step, side * near)

        repeat(low, high, body)

    def await_pair(chunk):
        def body(source):
            transfer(
                chunk, source * 2 + 1 - core, send_pair.at[chunk, source], pair, False
            ).wait_recv()

        repeat(0, line, body)

    def finish_sends(chunk):
        def body(source):
            for sign in (1, -1):
                origin = jnp.clip(source, first, last) if chunk == PANEL else source

                @pl.when(onward(sign) & (origin * sign <= spot * sign))
                def _():
                    along(chunk, source, sign, False).wait_send()

            @pl.when(active)
            def _():
                across(chunk, source, False).wait_send()

        if chunk == PANEL:

            def guarded(source):
                pl.when(active)(lambda: body(source))

            repeat(0, line, guarded)
        else:
            repeat(0, line, body)

    def own_copy(chunk):
        return pltpu.make_async_copy(own(chunk), full(chunk, me), own_sem.at[chunk])

    def spread(buffer, send, receive, who, offset):
        peer = lax.rem(section + offset, section_count)
        return pltpu.make_async_remote_copy(
            src_ref=buffer.at[section, who],
            dst_ref=buffer.at[section, who],
            send_sem=send.at[who, offset],
            recv_sem=receive.at[who, section],
            device_id={"section": peer},
            device_id_type=MESH,
        )

    def await_spread(buffer, send, receive, who):
        for offset in range(1, section_count):
            peer = lax.rem(section + offset, section_count)
            pltpu.make_async_remote_copy(
                src_ref=buffer.at[peer, who],
                dst_ref=buffer.at[peer, who],
                send_sem=send.at[who, offset],
                recv_sem=receive.at[who, peer],
                device_id={"section": peer},
                device_id_type=MESH,
            ).wait_recv()

    def to_host():
        return (
            pltpu.make_async_remote_copy(
                src_ref=rows_all.at[section, 0],
                dst_ref=rows_all.at[section, 1],
                send_sem=guest_send.at[0],
                recv_sem=guest_recv.at[0],
                device_id={"seq": host},
                device_id_type=MESH,
            ),
            pltpu.make_async_remote_copy(
                src_ref=gate_rows.at[0],
                dst_ref=gate_rows.at[1],
                send_sem=guest_send.at[1],
                recv_sem=guest_recv.at[1],
                device_id={"seq": host},
                device_id_type=MESH,
            ),
        )

    def give_back(half, target):
        return pltpu.make_async_remote_copy(
            src_ref=results.at[half],
            dst_ref=returned.at[half],
            send_sem=back_send.at[half],
            recv_sem=back_recv.at[half],
            device_id={"seq": target},
            device_id_type=MESH,
        )

    for slot in range(slots):
        number = chosen_ref[me * slots + slot]
        rows = tokens_ref[:BLOCK, :]
        gates = gate_ref[:1, :]
        for block in range(1, gate_ref.shape[0]):
            rows = jnp.where(
                jnp.full(rows.shape, number, jnp.int32) == block,
                tokens_ref[block * BLOCK : (block + 1) * BLOCK, :],
                rows,
            )
            gates = jnp.where(
                jnp.full(gates.shape, number, jnp.int32) == block,
                gate_ref[block : block + 1, :],
                gates,
            )
        rows_all[section, 0, pl.ds(slot * BLOCK, BLOCK), :] = rows
        gate_rows[0, pl.ds(slot, 1), :] = gates
    total = seq_count * capacity
    tiles, tile = key_slots.shape
    lane = lax.broadcasted_iota(jnp.int32, (1, tile), 1)

    def fill(index):
        key_slot = lane + index * tile
        for piece in range(tile // BLOCK):
            place = index * (tile // BLOCK) + piece
            within = lax.rem(place, slots)
            count = jnp.full((1, tile), count_ref[place // slots], jnp.int32)
            key_slot = jnp.where(
                (lane // BLOCK == piece) & (count <= within), total, key_slot
            )
        key_slots[pl.ds(index, 1), :] = key_slot

    repeat(0, tiles, fill)

    barrier = pltpu.get_barrier_semaphore()

    @pl.when(spot + 1 < line)
    def _():
        pl.semaphore_signal(barrier, inc=1, device_id={"seq": me + 2}, device_id_type=MESH)

    @pl.when(spot > 0)
    def _():
        pl.semaphore_signal(barrier, inc=1, device_id={"seq": me - 2}, device_id_type=MESH)

    pl.semaphore_signal(barrier, inc=1, device_id={"seq": pair}, device_id_type=MESH)
    for offset in range(1, section_count):
        peer = lax.rem(section + offset, section_count)
        pl.semaphore_signal(barrier, inc=1, device_id={"section": peer}, device_id_type=MESH)
    neighbours = jnp.where(spot + 1 < line, 1, 0) + jnp.where(spot > 0, 1, 0)
    pl.semaphore_wait(barrier, section_count + neighbours)

    weights_chunks = (KEY, VALUE, QUERY_A, QUERY_B, OUT_A, OUT_B)

    @pl.when(jnp.logical_not(active))
    def _():
        for copy in to_host():
            copy.start()
        for chunk in weights_chunks:
            begin(chunk, spot)

    def gate_column(who):
        wide = gate_rows[who]
        square = lax.broadcasted_iota(jnp.int32, (BLOCK, BLOCK), 0) == lax.broadcasted_iota(
            jnp.int32, (BLOCK, BLOCK), 1
        )
        return jnp.concatenate(
            [
                jnp.sum(jnp.where(square, wide[slot : slot + 1, :], 0.0), axis=1, keepdims=True)
                for slot in range(slots)
            ],
            axis=0,
        )

    def normalise(who):
        square_sum = jnp.zeros((capacity, 1), jnp.float32)
        for part in range(section_count):
            features = rows_all[part, who].astype(jnp.float32)
            square_sum += jnp.sum(features * features, axis=-1, keepdims=True)
        factor = lax.rsqrt(square_sum / depth + EPSILON)
        for part in range(section_count):
            cols = pl.ds(part * width, width)
            normed_ref[pl.ds(who * capacity, capacity), cols] = (
                rows_all[part, who].astype(jnp.float32) * factor * gain_ref[:, cols]
            ).astype(jnp.bfloat16)

    def attend(who, owner):
        scale = HEAD_DIM ** (-0.5)
        tall = lax.broadcasted_iota(jnp.int32, (ratio * capacity, 1), 0)
        query_slot = lax.rem(tall, capacity) + owner * capacity
        for group in range(groups):
            numer_ref[...] = jnp.zeros_like(numer_ref)
            denom_ref[...] = jnp.zeros_like(denom_ref)

            def fold(index):
                start = index * tile
                key_slot = key_slots[pl.ds(index, 1), :]
                rows = pl.ds(pl.multiple_of(start, tile), tile)
                keys = panel[rows, pl.ds(group * HEAD_DIM, HEAD_DIM)]
                values = panel[rows, pl.ds(kv_cols + group * HEAD_DIM, HEAD_DIM)]
                wide = queries_ref[who, pl.ds(group * ratio, ratio)].reshape(
                    ratio * capacity, HEAD_DIM
                )
                scores = (
                    lax.dot_general(
                        wide, keys, (((1,), (1,)), ((), ())), preferred_element_type=jnp.float32
                    )
                    * scale
                )
                weights = jnp.where(key_slot <= query_slot, jnp.exp(scores), 0.0)
                denom_ref[...] += jnp.sum(weights, axis=-1, keepdims=True)
                numer_ref[...] += jnp.dot(
                    weights.astype(jnp.bfloat16), values, preferred_element_type=jnp.float32
                )

            repeat(0, total // tile, fold)
            safe = jnp.where(denom_ref[...] > 0, denom_ref[...], 1.0)
            result = (numer_ref[...] / safe).astype(jnp.bfloat16)
            for head in range(ratio):
                cols = pl.ds((group * ratio + head) * HEAD_DIM, HEAD_DIM)
                heads_all[section, who, :, cols] = result[head * capacity : (head + 1) * capacity]

    def finish(who, half):
        update = jnp.zeros((capacity, half_o), jnp.float32)
        head_cols = heads_all.shape[3]
        for part in range(section_count):
            update += jnp.dot(
                heads_all[part, who],
                wo[half, pl.ds(part * head_cols, head_cols), :],
                preferred_element_type=jnp.float32,
            )
        cols = pl.ds(half * half_o, half_o)
        return (
            rows_all[section, who, :, cols].astype(jnp.float32) + gate_column(who) * update
        ).astype(out_ref.dtype)

    @pl.when(active)
    def _():
        begin(KEY, spot)
        begin(VALUE, spot)
        for offset in range(1, section_count):
            spread(rows_all, rows_send, rows_recv, 0, offset).start()

        @pl.when(has_guest)
        def _():
            for copy in to_host():
                copy.wait_recv()
            for offset in range(1, section_count):
                spread(rows_all, rows_send, rows_recv, 1, offset).start()

        for chunk in weights_chunks:
            own_copy(chunk).start()
        relay_all((KEY, VALUE), 1, 2, (1,))
        begin(QUERY_A, spot)
        begin(QUERY_B, spot)
        relay_all((KEY, VALUE), 1, 2, (-1,))
        relay_all((KEY, VALUE), 2, line)
        await_spread(rows_all, rows_send, rows_recv, 0)
        normalise(0)
        relay_all((QUERY_A, QUERY_B), 1, 2, (1,))

        @pl.when(has_guest)
        def _():
            await_spread(rows_all, rows_send, rows_recv, 1)
            normalise(1)

        for chunk in (KEY, VALUE):
            await_pair(chunk)
            own_copy(chunk).wait()
        for position, weight in enumerate((wk, wv)):
            sums = jnp.dot(
                normed_ref[...], weight[...], preferred_element_type=jnp.float32
            ).astype(jnp.bfloat16)
            cols = pl.ds(position * kv_cols, kv_cols)
            panel[rows_of(me, capacity), cols] = sums[:capacity]

            @pl.when(has_guest)
            def _():
                panel[rows_of(guest, capacity), cols] = sums[capacity:]

        begin(PANEL, spot)

        @pl.when(has_guest)
        def _():
            begin(GUEST_PANEL, guest_spot)

        begin(OUT_A, spot)
        begin(OUT_B, spot)
        relay_all((QUERY_A, QUERY_B), 1, 2, (-1,))
        relay_all((QUERY_A, QUERY_B), 2, line)
        relay_all((PANEL, GUEST_PANEL), 1, line)
        relay_all((OUT_A, OUT_B), 1, 2, (1,))
        heads_half = half_q // HEAD_DIM
        for half in range(2):
            await_pair(QUERY_A + half)
            own_copy(QUERY_A + half).wait()
            sums = jnp.dot(
                normed_ref[...], wq[half], preferred_element_type=jnp.float32
            ).astype(jnp.bfloat16)
            for who in range(2):
                for head in range(heads_half):
                    queries_ref[who, half * heads_half + head] = sums[
                        who * capacity : (who + 1) * capacity,
                        head * HEAD_DIM : (head + 1) * HEAD_DIM,
                    ]
        await_pair(PANEL)

        @pl.when(has_guest)
        def _():
            attend(1, guest)
            for offset in range(1, section_count):
                spread(heads_all, heads_send, heads_recv, 1, offset).start()

        attend(0, me)
        for offset in range(1, section_count):
            spread(heads_all, heads_send, heads_recv, 0, offset).start()
        relay_all((OUT_A, OUT_B), 1, 2, (-1,))
        relay_all((OUT_A, OUT_B), 2, line)
        for half in range(2):
            await_pair(OUT_A + half)
            own_copy(OUT_A + half).wait()

        @pl.when(has_guest)
        def _():
            await_spread(heads_all, heads_send, heads_recv, 1)
            for half in range(2):
                results[half] = finish(1, half)
                give_back(half, guest).start()

        await_spread(heads_all, heads_send, heads_recv, 0)
        for half in range(2):
            out_ref[:, pl.ds(half * half_o, half_o)] = finish(0, half)
        for offset in range(1, section_count):
            spread(rows_all, rows_send, rows_recv, 0, offset).wait_send()
            spread(heads_all, heads_send, heads_recv, 0, offset).wait_send()

        @pl.when(has_guest)
        def _():
            for offset in range(1, section_count):
                spread(rows_all, rows_send, rows_recv, 1, offset).wait_send()
                spread(heads_all, heads_send, heads_recv, 1, offset).wait_send()
            for half in range(2):
                give_back(half, guest).wait_send()

    for chunk in weights_chunks + (PANEL,):
        finish_sends(chunk)

    @pl.when(jnp.logical_not(active))
    def _():
        for copy in to_host():
            copy.wait_send()
        for half in range(2):
            give_back(half, host).wait_recv()
            out_ref[:, pl.ds(half * half_o, half_o)] = returned[half]


def put(tokens_ref, rows_ref, chosen_ref, count_ref, mixed_ref):
    me = lax.axis_index("seq")
    mixed_ref[...] = tokens_ref[...]
    slots = rows_ref.shape[0] // BLOCK
    for slot in range(slots):

        @pl.when(slot < count_ref[me])
        def _():
            start = pl.multiple_of(chosen_ref[me * slots + slot] * BLOCK, BLOCK)
            mixed_ref[pl.ds(start, BLOCK), :] = rows_ref[slot * BLOCK : (slot + 1) * BLOCK, :]


def local(
    tokens, norm_gain, w_query, w_key, w_value, w_out, router_gate, chosen_blocks, block_counts
):
    seq_count = lax.axis_size("seq")
    section_count = lax.axis_size("section")
    tok_rows, width = tokens.shape
    slots = chosen_blocks.shape[1]
    capacity = slots * BLOCK
    depth = section_count * width
    query_cols = w_query.shape[1]
    kv_cols = w_key.shape[1]
    ratio = HEADS // KV_HEADS
    line = seq_count // 2

    vmem = pl.BlockSpec(memory_space=pltpu.VMEM)
    smem = pl.BlockSpec(memory_space=pltpu.SMEM)
    anywhere = pl.BlockSpec(memory_space=pl.ANY)
    bf16 = jnp.bfloat16
    dma = pltpu.SemaphoreType.DMA
    tile = math.gcd(seq_count * capacity, 512)
    blocks = chosen_blocks.reshape(-1)
    new_rows = pl.pallas_call(
        functools.partial(kernel, seq_count, section_count),
        out_shape=jax.ShapeDtypeStruct((capacity, width), tokens.dtype),
        in_specs=[vmem] * 3 + [smem] * 2 + [anywhere] * 4,
        out_specs=vmem,
        scratch_shapes=[
            pltpu.VMEM((section_count, 2, capacity, width), bf16),
            pltpu.VMEM((2, slots, BLOCK), jnp.float32),
            pltpu.VMEM((2 * capacity, depth), bf16),
            pltpu.VMEM((depth, kv_cols), bf16),
            pltpu.VMEM((depth, kv_cols), bf16),
            pltpu.VMEM((2, depth, query_cols // 2), bf16),
            pltpu.VMEM((2, w_out.shape[0] * seq_count, w_out.shape[1] // 2), bf16),
            pltpu.VMEM((seq_count * capacity, 2 * kv_cols), bf16),
            pltpu.VMEM((2, query_cols // HEAD_DIM, capacity, HEAD_DIM), bf16),
            pltpu.VMEM((ratio * capacity, HEAD_DIM), jnp.float32),
            pltpu.VMEM((ratio * capacity, 1), jnp.float32),
            pltpu.VMEM((section_count, 2, capacity, query_cols), bf16),
            pltpu.VMEM((2, capacity, width // 2), bf16),
            pltpu.VMEM((2, capacity, width // 2), bf16),
            dma((7, seq_count)),
            dma((2, 7, line)),
            dma((7, line)),
            dma((6,)),
            dma((2, section_count)),
            dma((2, section_count)),
            dma((2, section_count)),
            dma((2, section_count)),
            dma((2,)),
            dma((2,)),
            dma((2,)),
            dma((2,)),
            pltpu.VMEM((seq_count * capacity // tile, tile), jnp.int32),
        ],
        compiler_params=pltpu.CompilerParams(collective_id=0, has_side_effects=True),
    )(
        tokens,
        norm_gain[None, :],
        router_gate.reshape(tok_rows // BLOCK, BLOCK),
        blocks,
        block_counts,
        w_query,
        w_key,
        w_value,
        w_out,
    )
    return pl.pallas_call(
        put,
        out_shape=jax.ShapeDtypeStruct(tokens.shape, tokens.dtype),
        in_specs=[vmem, vmem, smem, smem],
        out_specs=vmem,
    )(tokens, new_rows, blocks, block_counts)


def solution(mesh):
    return jax.shard_map(
        local,
        mesh=mesh,
        in_specs=(
            P("seq", "section"),
            P(),
            P("seq", "section"),
            P("seq", "section"),
            P("seq", "section"),
            P("seq", "section"),
            P("seq"),
            P(),
            P(),
        ),
        out_specs=P("seq", "section"),
        check_vma=False,
    )
```

profile of v0, /device:TPU:0, one launch (start us, length us, event | category | flops | bytes accessed | tf_op | source)
XLA Modules:
  0.0 52.7 jit_solution(2832289744355667759)
XLA Ops:
  0.0 50.8 %shard_map.91.rows_ref = bf16[128,512]{1,0:T(8,128)(2,1)} custom-call(bf16[512,512]{1,0:T(8,128)(2,1)} %tokens_ref.3, f32[1,2048]{1,0:T(1,128)} %bitcast.3, f32[4,128]{1,0:T(4,128)} %bitcast.4, s32[8]{0:T(128)} %bitcast.5, s32[8]{0:T(128)} %count_ref.3, bf16[256,512]{1,0:T(8,128)(2,1)} %wq_in.1, bf16[256,128]{1,0:T(8,128)(2,1)} %wk_in.1, ...), custom_call_target="tpu_custom_call" | custom-call | tf_op jit(solution)/shard_map/pallas_call | solution.py:556
  50.8 1.9 %shard_map.92 = bf16[512,512]{1,0:T(8,128)(2,1)} custom-call(bf16[512,512]{1,0:T(8,128)(2,1)} %tokens_ref.3, bf16[128,512]{1,0:T(8,128)(2,1)} %shard_map.91.rows_ref, s32[8]{0:T(128)} %bitcast.6, s32[8]{0:T(128)} %count_ref.3), custom_call_target="tpu_custom_call" | custom-call | tf_op jit(solution)/shard_map/pallas_call | solution.py:602
where the time goes:
time: 52.8 us; the launch traced here: 52.7 us
  Pallas kernels  52.7 us (100%)
    pallas_call x1, Pallas kernels, local(): pl.pallas_call(functools.partial(kernel, seq_count, section_count), out_s...  50.8 us
    pallas_call x1, Pallas kernels, local(): pl.pallas_call(put, out_shape=jax.ShapeDtypeStruct(tokens.shape, tokens.d...  1.91 us

commit v1 on v0

v1 whole, which is shorter than its diff:
```python
import functools
import math

import jax
import jax.numpy as jnp
from jax import lax
from jax.experimental import pallas as pl
from jax.experimental.pallas import tpu as pltpu
from jax.sharding import PartitionSpec as P

HEADS = 16
KV_HEADS = 4
HEAD_DIM = 128
BLOCK = 128
EPSILON = 1e-05
MESH = pl.DeviceIdType.MESH

KV, QUERY, OUT_A, OUT_B = range(4)
CHUNKS = (KV, QUERY, OUT_A, OUT_B)


def repeat(low, high, body):
    if high - low <= 4:
        for step in range(low, high):
            body(step)
    else:

        def wrapped(step, carry):
            body(step)
            return carry

        lax.fori_loop(low, high, wrapped, 0)


def kernel(
    seq_count,
    section_count,
    tile_spots,
    tokens_ref,
    gain_ref,
    gate_ref,
    chosen_ref,
    count_ref,
    wq_in,
    wk_in,
    wv_in,
    wo_in,
    out_ref,
    rows_all,
    gate_rows,
    normed_ref,
    wkv,
    wq,
    wo,
    panel,
    queries_ref,
    numer_ref,
    denom_ref,
    heads_all,
    results,
    returned,
    key_slots,
    weight_send,
    weight_recv,
    rows_send,
    rows_pair,
    rows_recv,
    gate_send,
    gate_recv,
    panel_line,
    panel_pair,
    panel_recv,
    heads_send,
    heads_pair,
    heads_recv,
    back_send,
    back_recv,
):
    me = lax.axis_index("seq")
    section = lax.axis_index("section")
    line = seq_count // 2
    spot = me // 2
    core = lax.rem(me, 2)
    pair = spot * 2 + 1 - core
    slots = chosen_ref.shape[0] // seq_count
    capacity, width = out_ref.shape
    chip_rows = 2 * capacity
    kv_cols = wk_in.shape[1]
    ratio = HEADS // KV_HEADS
    half_q = wq_in.shape[1] // 2
    heads_half = half_q // HEAD_DIM
    half_o = wo_in.shape[1] // 2
    part_o = half_o // 2
    depth = section_count * width
    first, last = 1, line - 2
    active = (spot >= first) & (spot <= last)
    has_guest = (spot == first) | (spot == last)
    near = jnp.where(spot * 2 < line, 1, -1)
    guest_spot = spot - near
    host_spot = spot + near
    spots = (spot, guest_spot)

    def for_who(body):
        body(0)
        pl.when(has_guest)(lambda: body(1))

    def host_of(place):
        if isinstance(place, int):
            return min(max(place, first), last)
        return jnp.clip(place, first, last)

    def rows_of(block, size):
        return pl.ds(pl.multiple_of(block * size, size), size)

    def remote(src, dst, send, receive, **device):
        return pltpu.make_async_remote_copy(
            src_ref=src,
            dst_ref=dst,
            send_sem=send,
            recv_sem=receive,
            device_id=device,
            device_id_type=MESH,
        )

    def others(body):
        for offset in range(1, section_count):
            body(offset, lax.rem(section + offset, section_count))

    def weight_from(chunk, half):
        if chunk == KV:
            return (wk_in, wv_in)[half]
        if chunk == QUERY:
            return wq_in.at[:, pl.ds(half * half_q, half_q)]
        return wo_in.at[:, pl.ds(half * half_o + (chunk - OUT_A) * part_o, part_o)]

    def weight_to(chunk, block):
        if chunk == KV:
            return wkv.at[rows_of(block, wk_in.shape[0]), :]
        if chunk == QUERY:
            return wq.at[rows_of(block, wq_in.shape[0]), :]
        return wo.at[chunk - OUT_A, rows_of(block, wo_in.shape[0]), :]

    def weight_copy(chunk, half, target):
        return remote(
            weight_from(chunk, half),
            weight_to(chunk, me),
            weight_send.at[chunk, target],
            weight_recv.at[chunk, me],
            seq=target,
        )

    def send_weight(chunk):
        def body(host):
            for half in range(2):
                target = host * 2 + half

                @pl.when(target != me)
                def _():
                    weight_copy(chunk, half, target).start()

                @pl.when(target == me)
                def _():
                    pltpu.make_async_copy(
                        weight_from(chunk, half), weight_to(chunk, me), weight_recv.at[chunk, me]
                    ).start()

        repeat(first, last + 1, body)

    def finish_weight(chunk):
        def body(host):
            for half in range(2):
                target = host * 2 + half

                @pl.when(target != me)
                def _():
                    weight_copy(chunk, half, target).wait_send()

        repeat(first, last + 1, body)

    def await_weight(chunk):
        def body(block):
            pltpu.make_async_copy(
                weight_to(chunk, block), weight_to(chunk, block), weight_recv.at[chunk, block]
            ).wait()

        for block in range(0, seq_count) if seq_count <= 8 else ():
            body(block)
        if seq_count > 8:
            repeat(0, seq_count, body)

    def rows_copy(part, place, send, **device):
        return remote(
            rows_all.at[part, place],
            rows_all.at[part, place],
            send,
            rows_recv.at[place, part],
            **device,
        )

    def rows_spread(who, offset, peer):
        return rows_copy(section, who * 2 + core, rows_send.at[who, offset], section=peer)

    def rows_to_pair(who, part):
        return rows_copy(part, who * 2 + core, rows_pair.at[who, part], seq=pair)

    def await_rows(part, place):
        rows_copy(part, place, rows_send.at[0, 0], seq=pair).wait_recv()

    def guest_copies():
        copies = [
            remote(
                rows_all.at[section, core],
                rows_all.at[section, 2 + core],
                rows_send.at[0, 0],
                rows_recv.at[2 + core, section],
                seq=host_spot * 2 + core,
            )
        ]
        for half in range(2):
            copies.append(
                remote(
                    gate_rows.at[core],
                    gate_rows.at[2 + core],
                    gate_send.at[half],
                    gate_recv.at[2 + core],
                    seq=host_spot * 2 + half,
                )
            )
        return copies

    def gate_copy(place):
        return remote(
            gate_rows.at[place], gate_rows.at[place], gate_send.at[0], gate_recv.at[place], seq=pair
        )

    def panel_copy(kind, place, send, target):
        piece = panel.at[kind, rows_of(place, chip_rows), :]
        return remote(piece, piece, send, panel_recv.at[kind, place], seq=target)

    def panel_to_pair(place):
        return panel_copy(core, place, panel_pair.at[place], pair)

    def panel_onward(who, host):
        return panel_copy(core, spots[who], panel_line.at[who, host], host * 2 + core)

    def later_hosts(body):
        def guarded(host):
            pl.when(host > spot)(lambda: body(host))

        repeat(first, last + 1, guarded)

    def await_panel(kind, place):
        panel_copy(kind, place, panel_pair.at[place], pair).wait_recv()

    def earlier_spots(body):
        def guarded(place):
            pl.when(host_of(place) < spot)(lambda: body(place))

        repeat(0, line, guarded)

    def heads_copy(part, half, who, send, **device):
        piece = heads_all.at[part, half, who]
        return remote(piece, piece, send, heads_recv.at[who, half, part], **device)

    def heads_spread(who, offset, peer):
        return heads_copy(section, core, who, heads_send.at[who, offset], section=peer)

    def heads_to_pair(who, part):
        return heads_copy(part, core, who, heads_pair.at[who, part], seq=pair)

    def await_heads(who, half, part):
        heads_copy(part, half, who, heads_send.at[0, 0], seq=pair).wait_recv()

    def give_back(place, part, target):
        return remote(
            results.at[place, part],
            returned.at[core, part],
            back_send.at[place, part],
            back_recv.at[core, part],
            seq=target,
        )

    def await_back(half, part):
        remote(
            returned.at[half, part],
            returned.at[half, part],
            back_send.at[0, part],
            back_recv.at[half, part],
            seq=pair,
        ).wait_recv()

    for slot in range(slots):
        number = chosen_ref[me * slots + slot]
        rows = tokens_ref[:BLOCK, :]
        gates = gate_ref[:1, :]
        for block in range(1, gate_ref.shape[0]):
            rows = jnp.where(
                jnp.full(rows.shape, number, jnp.int32) == block,
                tokens_ref[block * BLOCK : (block + 1) * BLOCK, :],
                rows,
            )
            gates = jnp.where(
                jnp.full(gates.shape, number, jnp.int32) == block,
                gate_ref[block : block + 1, :],
                gates,
            )
        rows_all[section, core, pl.ds(slot * BLOCK, BLOCK), :] = rows
        gate_rows[core, pl.ds(slot, 1), :] = gates

    barrier = pltpu.get_barrier_semaphore()

    def greet(other):
        @pl.when((other != me) & (active | (other >= first * 2) & (other < (last + 1) * 2)))
        def _():
            pl.semaphore_signal(barrier, inc=1, device_id={"seq": other}, device_id_type=MESH)

    for other in range(seq_count) if seq_count <= 8 else ():
        greet(other)
    if seq_count > 8:
        repeat(0, seq_count, greet)

    @pl.when(active)
    def _():
        others(
            lambda offset, peer: pl.semaphore_signal(
                barrier, inc=1, device_id={"section": peer}, device_id_type=MESH
            )
        )

    hosts = (last - first + 1) * 2
    pl.semaphore_wait(barrier, jnp.where(active, seq_count - 1 + section_count - 1, hosts))

    @pl.when(jnp.logical_not(active))
    def _():
        for copy in guest_copies():
            copy.start()
        for chunk in CHUNKS:
            send_weight(chunk)

    def gate_column(place):
        wide = gate_rows[place]
        square = lax.broadcasted_iota(jnp.int32, (BLOCK, BLOCK), 0) == lax.broadcasted_iota(
            jnp.int32, (BLOCK, BLOCK), 1
        )
        return jnp.concatenate(
            [
                jnp.sum(jnp.where(square, wide[slot : slot + 1, :], 0.0), axis=1, keepdims=True)
                for slot in range(slots)
            ],
            axis=0,
        )

    def normalise(place):
        square_sum = jnp.zeros((capacity, 1), jnp.float32)
        for part in range(section_count):
            features = rows_all[part, place].astype(jnp.float32)
            square_sum += jnp.sum(features * features, axis=-1, keepdims=True)
        factor = lax.rsqrt(square_sum / depth + EPSILON)
        for part in range(section_count):
            cols = pl.ds(part * width, width)
            normed_ref[rows_of(place, capacity), cols] = (
                rows_all[part, place].astype(jnp.float32) * factor * gain_ref[:, cols]
            ).astype(jnp.bfloat16)

    tile = tile_spots * chip_rows
    total = seq_count * capacity
    lane = lax.broadcasted_iota(jnp.int32, (1, tile), 1)

    def fill_slots(index):
        key_slot = lane + index * tile
        for piece in range(tile // BLOCK):
            place = index * (tile // BLOCK) + piece
            within = lax.rem(place, slots)
            count = jnp.full((1, tile), count_ref[place // slots], jnp.int32)
            key_slot = jnp.where((lane // BLOCK == piece) & (count <= within), total, key_slot)
        key_slots[pl.ds(index, 1), :] = key_slot

    bundle = min(ratio, heads_half)
    bundles = heads_half // bundle
    scale = HEAD_DIM ** (-0.5)

    def fold(who, index):
        tall = lax.broadcasted_iota(jnp.int32, (bundle * chip_rows, 1), 0)
        query_slot = lax.rem(tall, chip_rows) + spots[who] * chip_rows
        key_slot = key_slots[pl.ds(index, 1), :]
        rows = rows_of(index, tile)
        for number in range(bundles):
            if kv_cols == HEAD_DIM:
                cols = pl.ds(0, HEAD_DIM)
            else:
                cols = rows_of((core * heads_half + number * bundle) // ratio, HEAD_DIM)
            keys = panel[0, rows, cols]
            values = panel[1, rows, cols]
            wide = queries_ref[who, pl.ds(number * bundle, bundle)].reshape(
                bundle * chip_rows, HEAD_DIM
            )
            scores = (
                lax.dot_general(
                    wide, keys, (((1,), (1,)), ((), ())), preferred_element_type=jnp.float32
                )
                * scale
            )
            weights = jnp.where(key_slot <= query_slot, jnp.exp(scores), 0.0)
            denom_ref[who, number] += jnp.sum(weights, axis=-1, keepdims=True)
            numer_ref[who, number] += jnp.dot(
                weights.astype(jnp.bfloat16), values, preferred_element_type=jnp.float32
            )

    def settle(who):
        for number in range(bundles):
            denom = denom_ref[who, number]
            safe = jnp.where(denom > 0, denom, 1.0)
            result = (numer_ref[who, number] / safe).astype(jnp.bfloat16)
            for head in range(bundle):
                cols = pl.ds((number * bundle + head) * HEAD_DIM, HEAD_DIM)
                heads_all[section, core, who, :, cols] = result[
                    head * chip_rows : (head + 1) * chip_rows
                ]

    def finish(part):
        update = jnp.zeros((2 * chip_rows, part_o), jnp.float32)
        for source in range(section_count):
            for half in range(2):
                update += jnp.dot(
                    heads_all[source, half].reshape(2 * chip_rows, half_q),
                    wo[part, pl.ds((source * 2 + half) * half_q, half_q), :],
                    preferred_element_type=jnp.float32,
                )
        cols = pl.ds(pl.multiple_of(core * half_o + part * part_o, part_o), part_o)

        def settle_rows(who):
            for half in range(2):
                place = who * 2 + half
                results[place, part] = (
                    rows_all[section, place, :, cols].astype(jnp.float32)
                    + gate_column(place) * update[place * capacity : (place + 1) * capacity]
                ).astype(out_ref.dtype)
                target = spots[who] * 2 + half
                pl.when(target != me)(lambda: give_back(place, part, target).start())

        pl.when(has_guest)(lambda: settle_rows(1))
        settle_rows(0)

    @pl.when(active)
    def _():
        others(lambda offset, peer: rows_spread(0, offset, peer).start())
        send_weight(KV)
        rows_to_pair(0, section).start()
        gate_copy(core).start()
        send_weight(QUERY)

        @pl.when(has_guest)
        def _():
            await_rows(section, 2 + core)
            others(lambda offset, peer: rows_spread(1, offset, peer).start())
            rows_to_pair(1, section).start()

        repeat(0, line // tile_spots, fill_slots)
        numer_ref[...] = jnp.zeros_like(numer_ref)
        denom_ref[...] = jnp.zeros_like(denom_ref)

        def gather(who):
            def forward(offset, peer):
                await_rows(peer, who * 2 + core)
                rows_to_pair(who, peer).start()

            others(forward)
            normalise(who * 2 + core)
            for part in range(section_count):
                await_rows(part, who * 2 + 1 - core)
            normalise(who * 2 + 1 - core)

        for_who(gather)
        await_weight(KV)
        sums = jnp.dot(normed_ref[...], wkv[...], preferred_element_type=jnp.float32).astype(
            jnp.bfloat16
        )

        def offer(who):
            panel[core, rows_of(spots[who], chip_rows), :] = sums[
                who * chip_rows : (who + 1) * chip_rows
            ]
            panel_to_pair(spots[who]).start()
            later_hosts(lambda host: panel_onward(who, host).start())

        for_who(offer)
        send_weight(OUT_A)
        send_weight(OUT_B)
        await_weight(QUERY)
        sums = jnp.dot(normed_ref[...], wq[...], preferred_element_type=jnp.float32).astype(
            jnp.bfloat16
        )
        for who in range(2):
            for head in range(heads_half):
                queries_ref[who, head] = sums[
                    who * chip_rows : (who + 1) * chip_rows,
                    head * HEAD_DIM : (head + 1) * HEAD_DIM,
                ]
        for_who(lambda who: await_panel(1 - core, spots[who]))
        for_who(lambda who: fold(who, spots[who] // tile_spots))

        def relay(place):
            await_panel(core, place)
            panel_to_pair(place).start()

        earlier_spots(relay)
        earlier_spots(lambda place: await_panel(1 - core, place))

        def rest(who):
            def body(index, carry):
                fold(who, index)
                return carry

            lax.fori_loop(0, spots[who] // tile_spots, body, 0)
            settle(who)
            others(lambda offset, peer: heads_spread(who, offset, peer).start())
            heads_to_pair(who, section).start()

        for_who(rest)

        def pass_on(who):
            def forward(offset, peer):
                await_heads(who, core, peer)
                heads_to_pair(who, peer).start()

            others(forward)

        for_who(pass_on)

        def collect(who):
            for part in range(section_count):
                await_heads(who, 1 - core, part)

        for_who(collect)
        gate_copy(1 - core).wait_recv()

        @pl.when(has_guest)
        def _():
            for half in range(2):
                gate_copy(2 + half).wait_recv()

        for part in range(2):
            await_weight(OUT_A + part)
            finish(part)

        def drain(who):
            others(lambda offset, peer: rows_spread(who, offset, peer).wait_send())
            others(lambda offset, peer: heads_spread(who, offset, peer).wait_send())
            for part in range(section_count):
                rows_to_pair(who, part).wait_send()
                heads_to_pair(who, part).wait_send()
            panel_to_pair(spots[who]).wait_send()
            later_hosts(lambda host: panel_onward(who, host).wait_send())
            for half in range(2):
                target = spots[who] * 2 + half
                for part in range(2):
                    pl.when(target != me)(
                        lambda: give_back(who * 2 + half, part, target).wait_send()
                    )

        for_who(drain)
        gate_copy(core).wait_send()
        earlier_spots(lambda place: panel_to_pair(place).wait_send())
        for part in range(2):
            for half in range(2):
                cols = pl.ds(half * half_o + part * part_o, part_o)

                @pl.when(core == half)
                def _():
                    out_ref[:, cols] = results[half, part]

                @pl.when(core != half)
                def _():
                    await_back(half, part)
                    out_ref[:, cols] = returned[half, part]

    for chunk in CHUNKS:
        finish_weight(chunk)

    @pl.when(jnp.logical_not(active))
    def _():
        for copy in guest_copies():
            copy.wait_send()
        for part in range(2):
            for half in range(2):
                await_back(half, part)
                cols = pl.ds(half * half_o + part * part_o, part_o)
                out_ref[:, cols] = returned[half, part]


def put(tokens_ref, rows_ref, chosen_ref, count_ref, mixed_ref):
    me = lax.axis_index("seq")
    mixed_ref[...] = tokens_ref[...]
    slots = rows_ref.shape[0] // BLOCK
    for slot in range(slots):

        @pl.when(slot < count_ref[me])
        def _():
            start = pl.multiple_of(chosen_ref[me * slots + slot] * BLOCK, BLOCK)
            mixed_ref[pl.ds(start, BLOCK), :] = rows_ref[slot * BLOCK : (slot + 1) * BLOCK, :]


def local(
    tokens, norm_gain, w_query, w_key, w_value, w_out, router_gate, chosen_blocks, block_counts
):
    seq_count = lax.axis_size("seq")
    section_count = lax.axis_size("section")
    tok_rows, width = tokens.shape
    slots = chosen_blocks.shape[1]
    capacity = slots * BLOCK
    chip_rows = 2 * capacity
    depth = section_count * width
    half_q = w_query.shape[1] // 2
    heads_half = half_q // HEAD_DIM
    part_o = w_out.shape[1] // 4
    kv_cols = w_key.shape[1]
    line = seq_count // 2
    tile_spots = 2 if line == 4 else 1
    tile = tile_spots * chip_rows
    bundle = min(HEADS // KV_HEADS, heads_half)

    vmem = pl.BlockSpec(memory_space=pltpu.VMEM)
    smem = pl.BlockSpec(memory_space=pltpu.SMEM)
    anywhere = pl.BlockSpec(memory_space=pl.ANY)
    bf16 = jnp.bfloat16
    dma = pltpu.SemaphoreType.DMA
    blocks = chosen_blocks.reshape(-1)
    new_rows = pl.pallas_call(
        functools.partial(kernel, seq_count, section_count, tile_spots),
        out_shape=jax.ShapeDtypeStruct((capacity, width), tokens.dtype),
        in_specs=[vmem] * 3 + [smem] * 2 + [anywhere] * 4,
        out_specs=vmem,
        scratch_shapes=[
            pltpu.VMEM((section_count, 4, capacity, width), bf16),
            pltpu.VMEM((4, slots, BLOCK), jnp.float32),
            pltpu.VMEM((4 * capacity, depth), bf16),
            pltpu.VMEM((depth, kv_cols), bf16),
            pltpu.VMEM((depth, half_q), bf16),
            pltpu.VMEM((2, w_out.shape[0] * seq_count, part_o), bf16),
            pltpu.VMEM((2, seq_count * capacity, kv_cols), bf16),
            pltpu.VMEM((2, heads_half, chip_rows, HEAD_DIM), bf16),
            pltpu.VMEM((2, heads_half // bundle, bundle * chip_rows, HEAD_DIM), jnp.float32),
            pltpu.VMEM((2, heads_half // bundle, bundle * chip_rows, 1), jnp.float32),
            pltpu.VMEM((section_count, 2, 2, chip_rows, half_q), bf16),
            pltpu.VMEM((4, 2, capacity, part_o), bf16),
            pltpu.VMEM((2, 2, capacity, part_o), bf16),
            pltpu.VMEM((line // tile_spots, tile), jnp.int32),
            dma((len(CHUNKS), seq_count)),
            dma((len(CHUNKS), seq_count)),
            dma((2, section_count)),
            dma((2, section_count)),
            dma((4, section_count)),
            dma((2,)),
            dma((4,)),
            dma((2, line)),
            dma((line,)),
            dma((2, line)),
            dma((2, section_count)),
            dma((2, section_count)),
            dma((2, 2, section_count)),
            dma((4, 2)),
            dma((2, 2)),
        ],
        compiler_params=pltpu.CompilerParams(collective_id=0, has_side_effects=True),
    )(
        tokens,
        norm_gain[None, :],
        router_gate.reshape(tok_rows // BLOCK, BLOCK),
        blocks,
        block_counts,
        w_query,
        w_key,
        w_value,
        w_out,
    )
    return pl.pallas_call(
        put,
        out_shape=jax.ShapeDtypeStruct(tokens.shape, tokens.dtype),
        in_specs=[vmem, vmem, smem, smem],
        out_specs=vmem,
    )(tokens, new_rows, blocks, block_counts)


def solution(mesh):
    return jax.shard_map(
        local,
        mesh=mesh,
        in_specs=(
            P("seq", "section"),
            P(),
            P("seq", "section"),
            P("seq", "section"),
            P("seq", "section"),
            P("seq", "section"),
            P("seq"),
            P(),
            P(),
        ),
        out_specs=P("seq", "section"),
        check_vma=False,
    )
```

time: 52.8 us -> 55.2 us (1.045)
  the two profiles are of different devices: /device:TPU:0 before, /device:TPU:25 now
where the time goes in v1:
time: 55.2 us; the launch traced here: 55 us
  Pallas kernels  55 us (100%)
    pallas_call x1, Pallas kernels, local(): pl.pallas_call(functools.partial(kernel, seq_count, section_count, tile_s...  53.1 us
    pallas_call x1, Pallas kernels, local(): pl.pallas_call(put, out_shape=jax.ShapeDtypeStruct(tokens.shape, tokens.d...  1.91 us

profile of v1, /device:TPU:25, one launch (start us, length us, event | category | flops | bytes accessed | tf_op | source)
XLA Modules:
  0.0 55.0 jit_solution(11321800258996234608)
XLA Ops:
  0.0 53.1 %shard_map.91.rows_ref = bf16[128,512]{1,0:T(8,128)(2,1)} custom-call(bf16[512,512]{1,0:T(8,128)(2,1)} %tokens_ref.3, f32[1,2048]{1,0:T(1,128)} %bitcast.3, f32[4,128]{1,0:T(4,128)} %bitcast.4, s32[8]{0:T(128)} %bitcast.5, s32[8]{0:T(128)} %count_ref.3, bf16[256,512]{1,0:T(8,128)(2,1)} %wq_in.1, bf16[256,128]{1,0:T(8,128)(2,1)} %wk_in.1, ...), custom_call_target="tpu_custom_call" | custom-call | tf_op jit(solution)/shard_map/pallas_call | solution.py:628
  53.1 1.9 %shard_map.92 = bf16[512,512]{1,0:T(8,128)(2,1)} custom-call(bf16[512,512]{1,0:T(8,128)(2,1)} %tokens_ref.3, bf16[128,512]{1,0:T(8,128)(2,1)} %shard_map.91.rows_ref, s32[8]{0:T(128)} %bitcast.6, s32[8]{0:T(128)} %count_ref.3), custom_call_target="tpu_custom_call" | custom-call | tf_op jit(solution)/shard_map/pallas_call | solution.py:676

commit v2 on v1

v2 whole, which is shorter than its diff:
```python
import functools

import jax
import jax.numpy as jnp
from jax import lax
from jax.experimental import pallas as pl
from jax.experimental.pallas import tpu as pltpu
from jax.sharding import PartitionSpec as P

HEADS = 16
KV_HEADS = 4
HEAD_DIM = 128
BLOCK = 128
EPSILON = 1e-05
MESH = pl.DeviceIdType.MESH

KV, QUERY, OUT = range(3)


def repeat(low, high, body):
    if high - low <= 8:
        for step in range(low, high):
            body(step)
    else:

        def wrapped(step, carry):
            body(step)
            return carry

        lax.fori_loop(low, high, wrapped, 0)


def kernel(
    seq_count,
    section_count,
    tile_spots,
    tokens_hbm,
    gain_ref,
    gate_ref,
    chosen_ref,
    count_ref,
    wq_in,
    wk_in,
    wv_in,
    wo_in,
    out_ref,
    tokens_ref,
    rows_all,
    gate_rows,
    normed_ref,
    wkv,
    wq,
    wo,
    panel,
    queries_ref,
    numer_ref,
    denom_ref,
    heads_all,
    results,
    returned,
    key_slots,
    tokens_sem,
    weight_send,
    weight_recv,
    guest_send,
    rows_send,
    rows_pair,
    rows_recv,
    gate_send,
    gate_recv,
    panel_line,
    panel_pair,
    panel_recv,
    heads_send,
    heads_pair,
    heads_recv,
    back_send,
    back_recv,
):
    me = lax.axis_index("seq")
    section = lax.axis_index("section")
    line = seq_count // 2
    spot = me // 2
    core = lax.rem(me, 2)
    pair = spot * 2 + 1 - core
    slots = chosen_ref.shape[1] // seq_count
    capacity, width = out_ref.shape
    chip_rows = 2 * capacity
    host_rows = 2 * chip_rows
    kv_cols = wk_in.shape[1]
    ratio = HEADS // KV_HEADS
    half_q = wq_in.shape[1] // 2
    heads_half = half_q // HEAD_DIM
    half_o = wo_in.shape[1] // 2
    parts_o, _, part_o = wo.shape
    depth = section_count * width
    chunks = [(KV, 0)]
    chunks += [(QUERY, head) for head in range(heads_half)]
    chunks += [(OUT, part) for part in range(parts_o)]
    number_of = {chunk: number for number, chunk in enumerate(chunks)}
    first, last = 1, line - 2
    active = (spot >= first) & (spot <= last)
    has_guest = (spot == first) | (spot == last)
    near = jnp.where(spot * 2 < line, 1, -1)
    guest_spot = spot - near
    host_spot = spot + near
    spots = (spot, guest_spot)
    beside = section + 1 - 2 * lax.rem(section, 2)
    above = lax.rem(section + 2, section_count)
    across = section_count - 1 - section

    def for_who(body):
        body(0)
        pl.when(has_guest)(lambda: body(1))

    def host_of(place):
        if isinstance(place, int):
            return min(max(place, first), last)
        return jnp.clip(place, first, last)

    def rows_of(block, size):
        if isinstance(block, int):
            return pl.ds(block * size, size)
        return pl.ds(pl.multiple_of(block * size, size), size)

    def remote(src, dst, send, receive, **device):
        return pltpu.make_async_remote_copy(
            src_ref=src,
            dst_ref=dst,
            send_sem=send,
            recv_sem=receive,
            device_id=device,
            device_id_type=MESH,
        )

    def weight_from(chunk, half):
        kind, part = chunk
        if kind == KV:
            return (wk_in, wv_in)[half]
        if kind == QUERY:
            return wq_in.at[:, pl.ds(half * half_q + part * HEAD_DIM, HEAD_DIM)]
        return wo_in.at[:, pl.ds(half * half_o + part * part_o, part_o)]

    def weight_to(chunk, block):
        kind, part = chunk
        if kind == KV:
            return wkv.at[rows_of(block, wk_in.shape[0]), :]
        if kind == QUERY:
            return wq.at[part, rows_of(block, wq_in.shape[0]), :]
        return wo.at[part, rows_of(block, wo_in.shape[0]), :]

    def weight_copy(chunk, half, target):
        number = number_of[chunk]
        return remote(
            weight_from(chunk, half),
            weight_to(chunk, me),
            weight_send.at[number, target],
            weight_recv.at[number, me],
            seq=target,
        )

    def send_weight(chunk):
        def body(host):
            for half in range(2):
                target = host * 2 + half

                @pl.when(target != me)
                def _():
                    weight_copy(chunk, half, target).start()

                @pl.when(target == me)
                def _():
                    pltpu.make_async_copy(
                        weight_from(chunk, half),
                        weight_to(chunk, me),
                        weight_recv.at[number_of[chunk], me],
                    ).start()

        repeat(first, last + 1, body)

    def finish_weight(chunk):
        def body(host):
            for half in range(2):
                target = host * 2 + half

                @pl.when(target != me)
                def _():
                    weight_copy(chunk, half, target).wait_send()

        repeat(first, last + 1, body)

    def await_weight(chunk, low=0, high=seq_count):
        def body(block):
            piece = weight_to(chunk, block)
            pltpu.make_async_copy(piece, piece, weight_recv.at[number_of[chunk], block]).wait()

        repeat(low, high, body)

    class Gather:
        def __init__(self, piece, send, pair_send, receive):
            self.piece, self.send, self.pair_send, self.receive = piece, send, pair_send, receive

        def copy(self, part, half, send, **device):
            piece = self.piece(part, half)
            return remote(piece, piece, send, self.receive.at[part, half], **device)

        def await_part(self, part, half):
            self.copy(part, half, self.send.at[0], seq=pair).wait_recv()

        def to_pair(self, part, half):
            return self.copy(part, half, self.pair_send.at[part, half], seq=pair)

        def sends(self):
            return (
                self.copy(section, 0, self.send.at[0], section=beside),
                self.copy(section, 1, self.send.at[1], section=above),
                self.copy(section, 1, self.send.at[2], section=beside),
                self.copy(section, 0, self.send.at[3], section=above),
            )

        def passes(self):
            return (
                self.copy(beside, 0, self.send.at[4], section=above),
                self.copy(above, 1, self.send.at[5], section=beside),
            )

        def start(self, ready=False):
            if ready:
                self.await_part(section, 0)
                self.await_part(section, 1)
            for copy in self.sends():
                copy.start()
            for half in range(2):
                self.to_pair(section, half).start()

        def relay(self):
            for (part, half), onward in zip(((beside, 0), (above, 1)), self.passes()):
                self.await_part(part, half)
                onward.start()
                self.to_pair(part, half).start()

        def complete(self):
            for part, half in ((beside, 1), (above, 0), (across, 0), (across, 1)):
                self.await_part(part, half)
                self.to_pair(part, half).start()

        def drain(self):
            for copy in self.sends() + self.passes():
                copy.wait_send()
            for part in range(section_count):
                for half in range(2):
                    self.to_pair(part, half).wait_send()

    def await_from_pair(piece, receive):
        for part in range(section_count):
            for half in range(2):
                remote(
                    piece(part, half),
                    piece(part, half),
                    receive.at[part, half],
                    receive.at[part, half],
                    seq=pair,
                ).wait_recv()

    def rows_piece(place):
        return lambda part, half: rows_all.at[part, place, rows_of(half, capacity // 2), :]

    def rows_gather(who):
        place = who * 2 + core
        return Gather(
            rows_piece(place), rows_send.at[who], rows_pair.at[who], rows_recv.at[place]
        )

    def guest_copies():
        copies = []
        for half in range(2):
            rows = rows_of(half, capacity // 2)
            copies.append(
                remote(
                    rows_all.at[section, core, rows, :],
                    rows_all.at[section, 2 + core, rows, :],
                    guest_send.at[half],
                    rows_recv.at[2 + core, section, half],
                    seq=host_spot * 2 + core,
                )
            )
        for half in range(2):
            copies.append(
                remote(
                    gate_rows.at[core],
                    gate_rows.at[2 + core],
                    gate_send.at[half],
                    gate_recv.at[2 + core],
                    seq=host_spot * 2 + half,
                )
            )
        return copies

    def gate_copy(place):
        return remote(
            gate_rows.at[place], gate_rows.at[place], gate_send.at[0], gate_recv.at[place], seq=pair
        )

    def panel_copy(kind, place, send, target):
        piece = panel.at[kind, rows_of(place, chip_rows), :]
        return remote(piece, piece, send, panel_recv.at[kind, place], seq=target)

    def panel_to_pair(place):
        return panel_copy(core, place, panel_pair.at[place], pair)

    def panel_onward(who, host):
        return panel_copy(core, spots[who], panel_line.at[who, host], host * 2 + core)

    def later_hosts(body):
        def guarded(host):
            pl.when(host > spot)(lambda: body(host))

        repeat(first, last + 1, guarded)

    def await_panel(kind, place):
        panel_copy(kind, place, panel_pair.at[place], pair).wait_recv()

    def earlier_spots(body):
        def guarded(place):
            pl.when(host_of(place) < spot)(lambda: body(place))

        repeat(0, line, guarded)

    def heads_piece(half_core, head):
        return lambda part, half: heads_all.at[part, half_core, head, rows_of(half, chip_rows), :]

    def heads_gather(head):
        return Gather(
            heads_piece(core, head),
            heads_send.at[head],
            heads_pair.at[head],
            heads_recv.at[head, core],
        )

    def give_back(place, part, target):
        return remote(
            results.at[place, part],
            returned.at[core, part],
            back_send.at[place, part],
            back_recv.at[core, part],
            seq=target,
        )

    def await_back(half, part):
        remote(
            returned.at[half, part],
            returned.at[half, part],
            back_send.at[0, part],
            back_recv.at[half, part],
            seq=pair,
        ).wait_recv()

    barrier = pltpu.get_barrier_semaphore()
    load_tokens = pltpu.make_async_copy(tokens_hbm, tokens_ref, tokens_sem.at[0])
    load_tokens.start()

    def greet(other):
        @pl.when((other != me) & (active | (other >= first * 2) & (other < (last + 1) * 2)))
        def _():
            pl.semaphore_signal(barrier, inc=1, device_id={"seq": other}, device_id_type=MESH)

    repeat(0, seq_count, greet)

    @pl.when(active)
    def _():
        for peer in (beside, above):
            pl.semaphore_signal(barrier, inc=1, device_id={"section": peer}, device_id_type=MESH)

    def pick(row_ref, index):
        row = row_ref[...]
        lane = lax.broadcasted_iota(jnp.int32, row.shape, 1)
        return jnp.sum(jnp.where(lane == index, row, 0), axis=1, keepdims=True)

    load_tokens.wait()
    for slot in range(slots):
        number = pick(chosen_ref, me * slots + slot)
        rows = tokens_ref[:BLOCK, :]
        gates = gate_ref[:1, :]
        for block in range(1, gate_ref.shape[0]):
            rows = jnp.where(
                jnp.broadcast_to(number, rows.shape) == block,
                tokens_ref[block * BLOCK : (block + 1) * BLOCK, :],
                rows,
            )
            gates = jnp.where(
                jnp.broadcast_to(number, gates.shape) == block,
                gate_ref[block : block + 1, :],
                gates,
            )
        rows_all[section, core, pl.ds(slot * BLOCK, BLOCK), :] = rows
        gate_rows[core, pl.ds(slot, 1), :] = gates

    hosts = (last - first + 1) * 2
    pl.semaphore_wait(barrier, jnp.where(active, seq_count - 1 + 2, hosts))

    @pl.when(jnp.logical_not(active))
    def _():
        for copy in guest_copies():
            copy.start()
        for chunk in chunks:
            send_weight(chunk)

    def gate_column(place):
        wide = gate_rows[place]
        square = lax.broadcasted_iota(jnp.int32, (BLOCK, BLOCK), 0) == lax.broadcasted_iota(
            jnp.int32, (BLOCK, BLOCK), 1
        )
        return jnp.concatenate(
            [
                jnp.sum(jnp.where(square, wide[slot : slot + 1, :], 0.0), axis=1, keepdims=True)
                for slot in range(slots)
            ],
            axis=0,
        )

    def normalise(place):
        square_sum = jnp.zeros((capacity, 1), jnp.float32)
        for part in range(section_count):
            features = rows_all[part, place].astype(jnp.float32)
            square_sum += jnp.sum(features * features, axis=-1, keepdims=True)
        factor = lax.rsqrt(square_sum / depth + EPSILON)
        for part in range(section_count):
            cols = pl.ds(part * width, width)
            normed_ref[rows_of(place, capacity), cols] = (
                rows_all[part, place].astype(jnp.float32) * factor * gain_ref[:, cols]
            ).astype(jnp.bfloat16)

    tile = tile_spots * chip_rows
    total = seq_count * capacity
    lane = lax.broadcasted_iota(jnp.int32, (1, tile), 1)

    def fill_slots(index):
        key_slot = lane + index * tile
        for piece in range(tile // BLOCK):
            place = index * (tile // BLOCK) + piece
            within = lax.rem(place, slots)
            count = jnp.broadcast_to(pick(count_ref, place // slots), (1, tile))
            key_slot = jnp.where((lane // BLOCK == piece) & (count <= within), total, key_slot)
        key_slots[pl.ds(index, 1), :] = key_slot

    scale = HEAD_DIM ** (-0.5)

    def fold(head, index):
        tall = lax.broadcasted_iota(jnp.int32, (host_rows, 1), 0)
        base = jnp.where(tall < chip_rows, spot * chip_rows, guest_spot * chip_rows - chip_rows)
        query_slot = tall + base
        key_slot = key_slots[pl.ds(index, 1), :]
        rows = rows_of(index, tile)
        if kv_cols == HEAD_DIM:
            cols = pl.ds(0, HEAD_DIM)
        else:
            cols = rows_of((core * heads_half + head) // ratio, HEAD_DIM)
        scores = (
            lax.dot_general(
                queries_ref[head],
                panel[0, rows, cols],
                (((1,), (1,)), ((), ())),
                preferred_element_type=jnp.float32,
            )
            * scale
        )
        weights = jnp.where(key_slot <= query_slot, jnp.exp(scores), 0.0)
        denom_ref[head] += jnp.sum(weights, axis=-1, keepdims=True)
        numer_ref[head] += jnp.dot(
            weights.astype(jnp.bfloat16), panel[1, rows, cols], preferred_element_type=jnp.float32
        )

    def fold_range(head, low, high):
        def body(index, carry):
            fold(head, index)
            return carry

        lax.fori_loop(low, high, body, 0)

    def finish(part):
        update = jnp.zeros((host_rows, part_o), jnp.float32)
        blocks = half_q // wo_in.shape[0]
        for source in range(section_count):
            for half in range(2):
                number = source * 2 + half
                await_weight((OUT, part), number * blocks, (number + 1) * blocks)
                attended = jnp.concatenate(
                    [heads_all[source, half, head] for head in range(heads_half)], axis=-1
                )
                update += jnp.dot(
                    attended,
                    wo[part, pl.ds(number * half_q, half_q), :],
                    preferred_element_type=jnp.float32,
                )
        cols = pl.ds(pl.multiple_of(core * half_o + part * part_o, part_o), part_o)

        def settle_rows(who):
            for half in range(2):
                place = who * 2 + half
                results[place, part] = (
                    rows_all[section, place, :, cols].astype(jnp.float32)
                    + gate_column(place) * update[place * capacity : (place + 1) * capacity]
                ).astype(out_ref.dtype)
                target = spots[who] * 2 + half
                pl.when(target != me)(lambda: give_back(place, part, target).start())

        pl.when(has_guest)(lambda: settle_rows(1))
        settle_rows(0)

    @pl.when(active)
    def _():
        rows_gather(0).start()
        send_weight((KV, 0))
        gate_copy(core).start()
        send_weight((QUERY, 0))
        repeat(0, line // tile_spots, fill_slots)
        numer_ref[...] = jnp.zeros_like(numer_ref)
        denom_ref[...] = jnp.zeros_like(denom_ref)
        rows_gather(0).relay()
        pl.when(has_guest)(lambda: rows_gather(1).start(ready=True))
        rows_gather(0).complete()
        pl.when(has_guest)(lambda: rows_gather(1).relay())
        normalise(core)
        await_from_pair(rows_piece(1 - core), rows_recv.at[1 - core])
        normalise(1 - core)

        @pl.when(has_guest)
        def _():
            rows_gather(1).complete()
            normalise(2 + core)
            await_from_pair(rows_piece(3 - core), rows_recv.at[3 - core])
            normalise(3 - core)

        await_weight((KV, 0))
        sums = jnp.dot(normed_ref[...], wkv[...], preferred_element_type=jnp.float32).astype(
            jnp.bfloat16
        )

        def offer(who):
            panel[core, rows_of(spots[who], chip_rows), :] = sums[
                who * chip_rows : (who + 1) * chip_rows
            ]
            panel_to_pair(spots[who]).start()
            later_hosts(lambda host: panel_onward(who, host).start())

        for_who(offer)
        for chunk in chunks[2:]:
            send_weight(chunk)
        own_tile = spot // tile_spots
        farthest = jnp.where(has_guest, jnp.maximum(spot, guest_spot), spot)
        tiles = farthest // tile_spots + 1
        for head in range(heads_half):
            await_weight((QUERY, head))
            queries_ref[head] = jnp.dot(
                normed_ref[...], wq[head], preferred_element_type=jnp.float32
            ).astype(jnp.bfloat16)
            if head == 0:
                for_who(lambda who: await_panel(1 - core, spots[who]))
            fold(head, own_tile)
            if head == 0:

                def pass_on(place):
                    await_panel(core, place)
                    panel_to_pair(place).start()

                earlier_spots(pass_on)
                earlier_spots(lambda place: await_panel(1 - core, place))
            fold_range(head, 0, own_tile)
            fold_range(head, own_tile + 1, tiles)
            denom = denom_ref[head]
            safe = jnp.where(denom > 0, denom, 1.0)
            heads_all[section, core, head] = (numer_ref[head] / safe).astype(jnp.bfloat16)
            heads_gather(head).start()
            heads_gather(head).relay()

        for head in range(heads_half):
            heads_gather(head).complete()
        for head in range(heads_half):
            await_from_pair(heads_piece(1 - core, head), heads_recv.at[head, 1 - core])
        gate_copy(1 - core).wait_recv()

        @pl.when(has_guest)
        def _():
            for half in range(2):
                gate_copy(2 + half).wait_recv()

        for part in range(parts_o):
            finish(part)

        def drain(who):
            rows_gather(who).drain()
            panel_to_pair(spots[who]).wait_send()
            later_hosts(lambda host: panel_onward(who, host).wait_send())
            for half in range(2):
                target = spots[who] * 2 + half
                for part in range(parts_o):
                    pl.when(target != me)(
                        lambda: give_back(who * 2 + half, part, target).wait_send()
                    )

        for_who(drain)
        for head in range(heads_half):
            heads_gather(head).drain()
        gate_copy(core).wait_send()
        earlier_spots(lambda place: panel_to_pair(place).wait_send())
        for part in range(parts_o):
            for half in range(2):
                cols = pl.ds(half * half_o + part * part_o, part_o)

                @pl.when(core == half)
                def _():
                    out_ref[:, cols] = results[half, part]

                @pl.when(core != half)
                def _():
                    await_back(half, part)
                    out_ref[:, cols] = returned[half, part]

    for chunk in chunks:
        finish_weight(chunk)

    @pl.when(jnp.logical_not(active))
    def _():
        for copy in guest_copies():
            copy.wait_send()
        for part in range(parts_o):
            for half in range(2):
                await_back(half, part)
                cols = pl.ds(half * half_o + part * part_o, part_o)
                out_ref[:, cols] = returned[half, part]


def put(tokens_ref, rows_ref, chosen_ref, count_ref, mixed_ref):
    me = lax.axis_index("seq")
    mixed_ref[...] = tokens_ref[...]
    slots = rows_ref.shape[0] // BLOCK
    for slot in range(slots):

        @pl.when(slot < count_ref[me])
        def _():
            start = pl.multiple_of(chosen_ref[me * slots + slot] * BLOCK, BLOCK)
            mixed_ref[pl.ds(start, BLOCK), :] = rows_ref[slot * BLOCK : (slot + 1) * BLOCK, :]


def local(
    tokens, norm_gain, w_query, w_key, w_value, w_out, router_gate, chosen_blocks, block_counts
):
    seq_count = lax.axis_size("seq")
    section_count = lax.axis_size("section")
    tok_rows, width = tokens.shape
    slots = chosen_blocks.shape[1]
    capacity = slots * BLOCK
    host_rows = 4 * capacity
    depth = section_count * width
    heads_half = w_query.shape[1] // 2 // HEAD_DIM
    parts_o = 2
    part_o = w_out.shape[1] // 2 // parts_o
    kv_cols = w_key.shape[1]
    line = seq_count // 2
    tile_spots = 2 if line == 4 else 1
    tile = tile_spots * 2 * capacity
    chunk_count = 1 + heads_half + parts_o

    vmem = pl.BlockSpec(memory_space=pltpu.VMEM)
    smem = pl.BlockSpec(memory_space=pltpu.SMEM)
    anywhere = pl.BlockSpec(memory_space=pl.ANY)
    bf16 = jnp.bfloat16
    f32 = jnp.float32
    dma = pltpu.SemaphoreType.DMA
    blocks = chosen_blocks.reshape(-1)
    new_rows = pl.pallas_call(
        functools.partial(kernel, seq_count, section_count, tile_spots),
        out_shape=jax.ShapeDtypeStruct((capacity, width), tokens.dtype),
        in_specs=[anywhere] + [vmem] * 4 + [anywhere] * 4,
        out_specs=vmem,
        scratch_shapes=[
            pltpu.VMEM(tokens.shape, bf16),
            pltpu.VMEM((section_count, 4, capacity, width), bf16),
            pltpu.VMEM((4, slots, BLOCK), f32),
            pltpu.VMEM((host_rows, depth), bf16),
            pltpu.VMEM((depth, kv_cols), bf16),
            pltpu.VMEM((heads_half, depth, HEAD_DIM), bf16),
            pltpu.VMEM((parts_o, w_out.shape[0] * seq_count, part_o), bf16),
            pltpu.VMEM((2, seq_count * capacity, kv_cols), bf16),
            pltpu.VMEM((heads_half, host_rows, HEAD_DIM), bf16),
            pltpu.VMEM((heads_half, host_rows, HEAD_DIM), f32),
            pltpu.VMEM((heads_half, host_rows, 1), f32),
            pltpu.VMEM((section_count, 2, heads_half, host_rows, HEAD_DIM), bf16),
            pltpu.VMEM((4, parts_o, capacity, part_o), bf16),
            pltpu.VMEM((2, parts_o, capacity, part_o), bf16),
            pltpu.VMEM((line // tile_spots, tile), jnp.int32),
            dma((1,)),
            dma((chunk_count, seq_count)),
            dma((chunk_count, seq_count)),
            dma((2,)),
            dma((2, 6)),
            dma((2, section_count, 2)),
            dma((4, section_count, 2)),
            dma((2,)),
            dma((4,)),
            dma((2, line)),
            dma((line,)),
            dma((2, line)),
            dma((heads_half, 6)),
            dma((heads_half, section_count, 2)),
            dma((heads_half, 2, section_count, 2)),
            dma((4, parts_o)),
            dma((2, parts_o)),
        ],
        compiler_params=pltpu.CompilerParams(collective_id=0, has_side_effects=True),
    )(
        tokens,
        norm_gain[None, :],
        router_gate.reshape(tok_rows // BLOCK, BLOCK),
        blocks[None, :],
        block_counts[None, :],
        w_query,
        w_key,
        w_value,
        w_out,
    )
    return pl.pallas_call(
        put,
        out_shape=jax.ShapeDtypeStruct(tokens.shape, tokens.dtype),
        in_specs=[vmem, vmem, smem, smem],
        out_specs=vmem,
    )(tokens, new_rows, blocks, block_counts)


def solution(mesh):
    return jax.shard_map(
        local,
        mesh=mesh,
        in_specs=(
            P("seq", "section"),
            P(),
            P("seq", "section"),
            P("seq", "section"),
            P("seq", "section"),
            P("seq", "section"),
            P("seq"),
            P(),
            P(),
        ),
        out_specs=P("seq", "section"),
        check_vma=False,
    )
```

time: 55.2 us -> 52.8 us (0.957)
  Pallas kernels: 55 us -> 52.5 us
    pallas_call x1, Pallas kernels: 53.1 us -> 50.6 us  [local(): pl.pallas_call(functools.partial(kernel, seq_count, section_count, tile_s...]
where the time goes in v2:
time: 52.8 us; the launch traced here: 52.5 us
  Pallas kernels  52.5 us (99%)
    pallas_call x1, Pallas kernels, local(): pl.pallas_call(functools.partial(kernel, seq_count, section_count, tile_s...  50.6 us
    pallas_call x1, Pallas kernels, local(): pl.pallas_call(put, out_shape=jax.ShapeDtypeStruct(tokens.shape, tokens.d...  1.91 us

profile of v2, /device:TPU:25, one launch (start us, length us, event | category | flops | bytes accessed | tf_op | source)
XLA Modules:
  0.0 52.5 jit_solution(13967885643969644599)
XLA Ops:
  0.0 50.6 %shard_map.91.rows_ref = bf16[128,512]{1,0:T(8,128)(2,1)} custom-call(bf16[512,512]{1,0:T(8,128)(2,1)} %tokens_ref.1, f32[1,2048]{1,0:T(1,128)} %bitcast.5, f32[4,128]{1,0:T(4,128)} %bitcast.6, s32[1,8]{1,0:T(1,128)} %bitcast.7, s32[1,8]{1,0:T(1,128)} %bitcast.9, bf16[256,512]{1,0:T(8,128)(2,1)} %wq_in.1, bf16[256,128]{1,0:T(8,128)(2,1)} %wk_in.1, ...), custom_call_target="tpu_custom_call" | custom-call | tf_op jit(solution)/shard_map/pallas_call | solution.py:671
  50.6 1.9 %shard_map.92 = bf16[512,512]{1,0:T(8,128)(2,1)} custom-call(bf16[512,512]{1,0:T(8,128)(2,1)} %tokens_ref.1, bf16[128,512]{1,0:T(8,128)(2,1)} %shard_map.91.rows_ref, s32[8]{0:T(128)} %bitcast.8, s32[8]{0:T(128)} %count_ref.1), custom_call_target="tpu_custom_call" | custom-call | tf_op jit(solution)/shard_map/pallas_call | solution.py:722

commit v3 on v2

v3 whole, which is shorter than its diff:
```python
import functools

import jax
import jax.numpy as jnp
from jax import lax
from jax.experimental import pallas as pl
from jax.experimental.pallas import tpu as pltpu
from jax.sharding import PartitionSpec as P

HEADS = 16
KV_HEADS = 4
HEAD_DIM = 128
BLOCK = 128
EPSILON = 1e-05
MESH = pl.DeviceIdType.MESH

KV, QUERY, OUT = range(3)


def chunks_of(heads_half, parts_o):
    chunks = [(KV, 0)]
    chunks += [(QUERY, head) for head in range(heads_half)]
    chunks += [(OUT, part) for part in range(parts_o)]
    return chunks


def repeat(low, high, body):
    if high - low <= 8:
        for step in range(low, high):
            body(step)
    else:

        def wrapped(step, carry):
            body(step)
            return carry

        lax.fori_loop(low, high, wrapped, 0)


def kernel(
    seq_count,
    section_count,
    tile_spots,
    tokens_hbm,
    gain_ref,
    gate_ref,
    chosen_ref,
    count_ref,
    wq_in,
    wk_in,
    wv_in,
    wo_in,
    mixed_ref,
    out_ref,
    rows_all,
    gate_rows,
    normed_ref,
    wkv,
    wq,
    wo,
    panel,
    queries_ref,
    numer_ref,
    denom_ref,
    heads_all,
    results,
    returned,
    key_slots,
    tokens_sem,
    weight_send,
    weight_recv,
    guest_send,
    rows_send,
    rows_recv,
    gate_send,
    gate_recv,
    panel_line,
    panel_pair,
    panel_recv,
    heads_send,
    heads_recv,
    back_send,
    back_recv,
):
    me = lax.axis_index("seq")
    section = lax.axis_index("section")
    line = seq_count // 2
    spot = me // 2
    core = lax.rem(me, 2)
    pair = spot * 2 + 1 - core
    slots = chosen_ref.shape[1] // seq_count
    capacity, width = out_ref.shape
    chip_rows = 2 * capacity
    host_rows = 2 * chip_rows
    kv_cols = wk_in.shape[1]
    ratio = HEADS // KV_HEADS
    half_q = wq_in.shape[1] // 2
    heads_half = half_q // HEAD_DIM
    half_o = wo_in.shape[1] // 2
    parts_o, _, _, part_o = wo.shape
    depth = section_count * width
    chunks = chunks_of(heads_half, parts_o)
    number_of = {chunk: number for number, chunk in enumerate(chunks)}
    first, last = 1, line - 2
    hosts = last - first + 1
    active = (spot >= first) & (spot <= last)
    has_guest = (spot == first) | (spot == last)
    near = jnp.where(spot * 2 < line, 1, -1)
    guest_spot = spot - near
    host_spot = spot + near
    spots = (spot, guest_spot)
    beside = section + 1 - 2 * lax.rem(section, 2)
    above = lax.rem(section + 2, section_count)
    across = section_count - 1 - section

    def host_of(place):
        if isinstance(place, int):
            return min(max(place, first), last)
        return jnp.clip(place, first, last)

    def rows_of(block, size):
        if isinstance(block, int):
            return pl.ds(block * size, size)
        return pl.ds(pl.multiple_of(block * size, size), size)

    def remote(src, dst, send, receive, **device):
        return pltpu.make_async_remote_copy(
            src_ref=src,
            dst_ref=dst,
            send_sem=send,
            recv_sem=receive,
            device_id=device,
            device_id_type=MESH,
        )

    def await_bytes(ref, sem):
        pltpu.make_async_copy(ref, ref, sem).wait()

    def weight_from(chunk, half):
        kind, part = chunk
        if kind == KV:
            return (wk_in, wv_in)[half]
        if kind == QUERY:
            return wq_in.at[:, pl.ds(half * half_q + part * HEAD_DIM, HEAD_DIM)]
        return wo_in.at[:, pl.ds(half * half_o + part * part_o, part_o)]

    def weight_to(chunk, low, count):
        kind, part = chunk
        blocks = pl.ds(low, count)
        if kind == KV:
            return wkv.at[blocks]
        if kind == QUERY:
            return wq.at[part, blocks]
        return wo.at[part, blocks]

    def weight_copy(chunk, half, target):
        number = number_of[chunk]
        return remote(
            weight_from(chunk, half),
            weight_to(chunk, me, 1).at[0],
            weight_send.at[number],
            weight_recv.at[number],
            seq=target,
        )

    def send_weight(chunk):
        def body(host):
            for half in range(2):
                target = host * 2 + half

                @pl.when(target != me)
                def _():
                    weight_copy(chunk, half, target).start()

                @pl.when(target == me)
                def _():
                    pltpu.make_async_copy(
                        weight_from(chunk, half),
                        weight_to(chunk, me, 1).at[0],
                        weight_recv.at[number_of[chunk]],
                    ).start()

        repeat(first, last + 1, body)

    def receive_weight(chunk):
        await_bytes(weight_to(chunk, 0, seq_count), weight_recv.at[number_of[chunk]])

    def finish_weight(chunk, count):
        await_bytes(weight_to(chunk, 0, count), weight_send.at[number_of[chunk]])

    class Gather:
        def __init__(self, at, place, other, rows, send, receive):
            self.at, self.place, self.other, self.rows = at, place, other, rows
            self.send, self.receive = send, receive

        def copy(self, part, half, send, receive, **device):
            piece = self.at(pl.ds(part, 1), self.place).at[0].at[rows_of(half, self.rows)]
            return remote(piece, piece, send, receive, **device)

        def send_part(self, part, half, peer):
            receive = self.receive.at[part * 2 + half]
            self.copy(part, half, self.send.at[0], receive, section=peer).start()

        def await_part(self, part, half):
            receive = self.receive.at[part * 2 + half]
            self.copy(part, half, self.send.at[0], receive, seq=pair).wait_recv()

        def to_pair(self, part, half):
            receive = self.receive.at[section_count * 2]
            self.copy(part, half, self.send.at[1], receive, seq=pair).start()

        def start(self, ready=False):
            if ready:
                self.await_part(section, 0)
            self.send_part(section, 0, beside)
            if ready:
                self.await_part(section, 1)
            self.send_part(section, 1, above)
            self.send_part(section, 1, beside)
            self.send_part(section, 0, above)
            self.to_pair(section, 0)
            self.to_pair(section, 1)

        def relay(self):
            self.await_part(beside, 0)
            self.send_part(beside, 0, above)
            self.to_pair(beside, 0)
            self.await_part(above, 1)
            self.send_part(above, 1, beside)
            self.to_pair(above, 1)

        def near(self):
            for part, half in ((beside, 1), (above, 0)):
                self.await_part(part, half)
                self.to_pair(part, half)

        def far(self):
            for half in range(2):
                self.await_part(across, half)
                self.to_pair(across, half)

        def await_pair(self):
            everything = self.at(pl.ds(0, section_count), self.other)
            await_bytes(everything, self.receive.at[section_count * 2])

        def drain(self):
            await_bytes(self.at(pl.ds(0, 3), self.place), self.send.at[0])
            await_bytes(self.at(pl.ds(0, section_count), self.place), self.send.at[1])

    def rows_gather(who):
        return Gather(
            lambda parts, place: rows_all.at[place, parts],
            who * 2 + core,
            who * 2 + 1 - core,
            capacity // 2,
            rows_send.at[who],
            rows_recv.at[who],
        )

    def guest_copies():
        copies = []
        for half in range(2):
            rows = rows_of(half, capacity // 2)
            copies.append(
                remote(
                    rows_all.at[core, section, rows, :],
                    rows_all.at[2 + core, section, rows, :],
                    guest_send.at[0],
                    rows_recv.at[1, section * 2 + half],
                    seq=host_spot * 2 + core,
                )
            )
        for half in range(2):
            copies.append(
                remote(
                    gate_rows.at[core],
                    gate_rows.at[2 + core],
                    gate_send.at[0],
                    gate_recv.at[1],
                    seq=host_spot * 2 + half,
                )
            )
        return copies

    def gate_copy(place):
        return remote(
            gate_rows.at[place], gate_rows.at[place], gate_send.at[0], gate_recv.at[0], seq=pair
        )

    def panel_copy(kind, place, send, target):
        piece = panel.at[kind, rows_of(place, chip_rows), :]
        return remote(piece, piece, send, panel_recv.at[kind, place], seq=target)

    def panel_to_pair(place):
        return panel_copy(core, place, panel_pair.at[place], pair)

    def panel_onward(who, host):
        return panel_copy(core, spots[who], panel_line.at[who, host - first], host * 2 + core)

    def later_hosts(body):
        def guarded(host):
            pl.when(host > spot)(lambda: body(host))

        repeat(first + 1, last + 1, guarded)

    def await_panel(kind, place):
        panel_copy(kind, place, panel_pair.at[place], pair).wait_recv()

    def earlier_spots(body):
        def guarded(step):
            place = last - 1 - step
            pl.when(host_of(place) < spot)(lambda: body(place))

        repeat(0, last, guarded)

    def heads_gather(head):
        return Gather(
            lambda parts, place: heads_all.at[place, head, parts],
            core,
            1 - core,
            chip_rows,
            heads_send.at[head],
            heads_recv.at[head],
        )

    def give_back(place, part, target):
        return remote(
            results.at[place, part],
            returned.at[core, part],
            back_send.at[0],
            back_recv.at[part],
            seq=target,
        )

    barrier = pltpu.get_barrier_semaphore()
    load_tokens = pltpu.make_async_copy(tokens_hbm, mixed_ref, tokens_sem.at[0])
    load_tokens.start()

    def greet(other):
        @pl.when((other != me) & (active | (other >= first * 2) & (other < (last + 1) * 2)))
        def _():
            pl.semaphore_signal(barrier, inc=1, device_id={"seq": other}, device_id_type=MESH)

    repeat(0, seq_count, greet)

    @pl.when(active)
    def _():
        for peer in (beside, above):
            pl.semaphore_signal(barrier, inc=1, device_id={"section": peer}, device_id_type=MESH)

    def pick(row_ref, index):
        row = row_ref[...]
        lane = lax.broadcasted_iota(jnp.int32, row.shape, 1)
        return jnp.sum(jnp.where(lane == index, row, 0), axis=1, keepdims=True)

    load_tokens.wait()
    for slot in range(slots):
        number = pick(chosen_ref, me * slots + slot)
        rows = mixed_ref[:BLOCK, :]
        gates = gate_ref[:1, :]
        for block in range(1, gate_ref.shape[0]):
            rows = jnp.where(
                jnp.broadcast_to(number, rows.shape) == block,
                mixed_ref[block * BLOCK : (block + 1) * BLOCK, :],
                rows,
            )
            gates = jnp.where(
                jnp.broadcast_to(number, gates.shape) == block,
                gate_ref[block : block + 1, :],
                gates,
            )
        rows_all[core, section, pl.ds(slot * BLOCK, BLOCK), :] = rows
        gate_rows[core, pl.ds(slot, 1), :] = gates

    pl.semaphore_wait(barrier, jnp.where(active, seq_count - 1 + 2, hosts * 2))

    @pl.when(jnp.logical_not(active))
    def _():
        for copy in guest_copies():
            copy.start()
        for chunk in chunks:
            send_weight(chunk)

    def gate_column(place):
        wide = gate_rows[place]
        square = lax.broadcasted_iota(jnp.int32, (BLOCK, BLOCK), 0) == lax.broadcasted_iota(
            jnp.int32, (BLOCK, BLOCK), 1
        )
        return jnp.concatenate(
            [
                jnp.sum(jnp.where(square, wide[slot : slot + 1, :], 0.0), axis=1, keepdims=True)
                for slot in range(slots)
            ],
            axis=0,
        )

    def normalise(place):
        square_sum = jnp.zeros((capacity, 1), jnp.float32)
        for part in range(section_count):
            features = rows_all[place, part].astype(jnp.float32)
            square_sum += jnp.sum(features * features, axis=-1, keepdims=True)
        factor = lax.rsqrt(square_sum / depth + EPSILON)
        for part in range(section_count):
            cols = pl.ds(part * width, width)
            normed_ref[rows_of(place, capacity), cols] = (
                rows_all[place, part].astype(jnp.float32) * factor * gain_ref[:, cols]
            ).astype(jnp.bfloat16)

    tile = tile_spots * chip_rows
    total = seq_count * capacity
    lane = lax.broadcasted_iota(jnp.int32, (1, tile), 1)

    def fill_slots(index):
        key_slot = lane + index * tile
        for piece in range(tile // BLOCK):
            place = index * (tile // BLOCK) + piece
            within = lax.rem(place, slots)
            count = jnp.broadcast_to(pick(count_ref, place // slots), (1, tile))
            key_slot = jnp.where((lane // BLOCK == piece) & (count <= within), total, key_slot)
        key_slots[pl.ds(index, 1), :] = key_slot

    scale = HEAD_DIM ** (-0.5)

    def offer(who):
        panel[core, rows_of(spots[who], chip_rows), :] = jnp.dot(
            normed_ref[rows_of(who, chip_rows), :],
            wkv[...].reshape(depth, kv_cols),
            preferred_element_type=jnp.float32,
        ).astype(jnp.bfloat16)
        panel_to_pair(spots[who]).start()
        later_hosts(lambda host: panel_onward(who, host).start())

    def ask(head):
        for who in range(2):
            queries_ref[head, rows_of(who, chip_rows), :] = jnp.dot(
                normed_ref[rows_of(who, chip_rows), :],
                wq[head].reshape(depth, HEAD_DIM),
                preferred_element_type=jnp.float32,
            ).astype(jnp.bfloat16)

    def fold(head, index):
        tall = lax.broadcasted_iota(jnp.int32, (host_rows, 1), 0)
        base = jnp.where(tall < chip_rows, spot * chip_rows, guest_spot * chip_rows - chip_rows)
        query_slot = tall + base
        key_slot = key_slots[pl.ds(index, 1), :]
        rows = rows_of(index, tile)
        if kv_cols == HEAD_DIM:
            cols = pl.ds(0, HEAD_DIM)
        else:
            cols = rows_of((core * heads_half + head) // ratio, HEAD_DIM)
        scores = (
            lax.dot_general(
                queries_ref[head],
                panel[0, rows, cols],
                (((1,), (1,)), ((), ())),
                preferred_element_type=jnp.float32,
            )
            * scale
        )
        weights = jnp.where(key_slot <= query_slot, jnp.exp(scores), 0.0)
        denom_ref[head] += jnp.sum(weights, axis=-1, keepdims=True)
        numer_ref[head] += jnp.dot(
            weights.astype(jnp.bfloat16), panel[1, rows, cols], preferred_element_type=jnp.float32
        )

    def fold_range(head, low, high):
        def body(index, carry):
            fold(head, index)
            return carry

        lax.fori_loop(low, high, body, 0)

    def settle(head):
        denom = denom_ref[head]
        safe = jnp.where(denom > 0, denom, 1.0)
        heads_all[core, head, section] = (numer_ref[head] / safe).astype(jnp.bfloat16)

    def finish(who, part):
        attended = [
            heads_all[half, head, source, rows_of(who, chip_rows), :]
            for source in range(section_count)
            for half in range(2)
            for head in range(heads_half)
        ]
        update = jnp.dot(
            jnp.concatenate(attended, axis=-1),
            wo[part].reshape(-1, part_o),
            preferred_element_type=jnp.float32,
        )
        cols = pl.ds(pl.multiple_of(core * half_o + part * part_o, part_o), part_o)
        for half in range(2):
            place = who * 2 + half
            fresh = (
                rows_all[place, section, :, cols].astype(jnp.float32)
                + gate_column(place) * update[half * capacity : (half + 1) * capacity]
            ).astype(out_ref.dtype)
            target = spots[who] * 2 + half
            if who == 0:
                pl.when(target == me)(lambda: out_ref.__setitem__((slice(None), cols), fresh))

            @pl.when(target != me)
            def _():
                results[place, part] = fresh
                give_back(place, part, target).start()

    early = 2

    @pl.when(active)
    def _():
        rows_gather(0).start()
        for chunk in chunks[:early]:
            send_weight(chunk)

        @pl.when(spot == last)
        def _():
            for chunk in chunks[early:]:
                send_weight(chunk)

        gate_copy(core).start()
        repeat(0, line // tile_spots, fill_slots)
        numer_ref[...] = jnp.zeros_like(numer_ref)
        denom_ref[...] = jnp.zeros_like(denom_ref)
        rows_gather(0).relay()
        pl.when(has_guest)(lambda: rows_gather(1).start(ready=True))
        rows_gather(0).near()
        rows_gather(0).far()
        pl.when(has_guest)(lambda: rows_gather(1).relay())
        normalise(core)
        rows_gather(0).await_pair()
        normalise(1 - core)
        receive_weight(chunks[0])
        offer(0)
        @pl.when(has_guest)
        def _():
            rows_gather(1).near()
            rows_gather(1).far()
            normalise(2 + core)
            rows_gather(1).await_pair()
            normalise(3 - core)
            offer(1)

        @pl.when(spot != last)
        def _():
            for chunk in chunks[early:]:
                send_weight(chunk)

        own_tile = spot // tile_spots
        farthest = jnp.where(has_guest, jnp.maximum(spot, guest_spot), spot)
        tiles = farthest // tile_spots + 1
        for head in range(heads_half):
            receive_weight((QUERY, head))
            ask(head)
            if head == 0:
                await_panel(1 - core, spot)
                pl.when(has_guest)(lambda: await_panel(1 - core, guest_spot))
            fold(head, own_tile)
            if head == 0:

                def pass_on(place):
                    await_panel(core, place)
                    panel_to_pair(place).start()

                earlier_spots(pass_on)
                earlier_spots(lambda place: await_panel(1 - core, place))
            fold_range(head, 0, own_tile)
            fold_range(head, own_tile + 1, tiles)
            settle(head)
            heads_gather(head).start()
            if head > 0:
                heads_gather(head - 1).relay()

        heads_gather(heads_half - 1).relay()
        gate_copy(1 - core).wait_recv()
        pl.when(has_guest)(lambda: await_bytes(gate_rows.at[pl.ds(2, 2)], gate_recv.at[1]))
        for head in range(heads_half):
            heads_gather(head).near()
        for head in range(heads_half):
            heads_gather(head).far()
        for head in range(heads_half):
            heads_gather(head).await_pair()
        for part in range(parts_o):
            receive_weight((OUT, part))
            pl.when(has_guest)(lambda: finish(1, part))
            finish(0, part)

        rows_gather(0).drain()
        for head in range(heads_half):
            heads_gather(head).drain()
        await_bytes(gate_rows.at[pl.ds(0, 1)], gate_send.at[0])
        panel_to_pair(spot).wait_send()
        later_hosts(lambda host: panel_onward(0, host).wait_send())
        earlier_spots(lambda place: panel_to_pair(place).wait_send())

        @pl.when(has_guest)
        def _():
            rows_gather(1).drain()
            panel_to_pair(guest_spot).wait_send()
            later_hosts(lambda host: panel_onward(1, host).wait_send())
            await_bytes(results.at[pl.ds(0, 3)], back_send.at[0])

        @pl.when(jnp.logical_not(has_guest))
        def _():
            await_bytes(results.at[pl.ds(0, 1)], back_send.at[0])

        for chunk in chunks:
            finish_weight(chunk, hosts * 2 - 1)
        for part in range(parts_o):
            cols = pl.ds(pl.multiple_of((1 - core) * half_o + part * part_o, part_o), part_o)
            await_bytes(returned.at[1 - core, part], back_recv.at[part])
            out_ref[:, cols] = returned[1 - core, part]

    @pl.when(jnp.logical_not(active))
    def _():
        await_bytes(rows_all.at[core, section], guest_send.at[0])
        await_bytes(gate_rows.at[pl.ds(0, 2)], gate_send.at[0])
        for chunk in chunks:
            finish_weight(chunk, hosts * 2)
        for part in range(parts_o):
            await_bytes(returned.at[pl.ds(0, 2), part], back_recv.at[part])
            for half in range(2):
                cols = pl.ds(half * half_o + part * part_o, part_o)
                out_ref[:, cols] = returned[half, part]

    for slot in range(slots):
        number = pick(chosen_ref, me * slots + slot)
        count = pick(count_ref, me)
        number = jnp.where(count > slot, number, gate_ref.shape[0])
        fresh = out_ref[slot * BLOCK : (slot + 1) * BLOCK, :]
        for block in range(gate_ref.shape[0]):
            rows = pl.ds(block * BLOCK, BLOCK)
            mixed_ref[rows, :] = jnp.where(
                jnp.broadcast_to(number, fresh.shape) == block, fresh, mixed_ref[rows, :]
            )


def local(
    tokens, norm_gain, w_query, w_key, w_value, w_out, router_gate, chosen_blocks, block_counts
):
    seq_count = lax.axis_size("seq")
    section_count = lax.axis_size("section")
    tok_rows, width = tokens.shape
    slots = chosen_blocks.shape[1]
    capacity = slots * BLOCK
    host_rows = 4 * capacity
    depth = section_count * width
    heads_half = w_query.shape[1] // 2 // HEAD_DIM
    parts_o = 2
    part_o = w_out.shape[1] // 2 // parts_o
    kv_cols = w_key.shape[1]
    line = seq_count // 2
    tile_spots = 2 if line == 4 else 1
    tile = tile_spots * 2 * capacity
    chunk_count = len(chunks_of(heads_half, parts_o))

    vmem = pl.BlockSpec(memory_space=pltpu.VMEM)
    anywhere = pl.BlockSpec(memory_space=pl.ANY)
    bf16 = jnp.bfloat16
    f32 = jnp.float32
    dma = pltpu.SemaphoreType.DMA
    blocks = chosen_blocks.reshape(-1)
    return pl.pallas_call(
        functools.partial(kernel, seq_count, section_count, tile_spots),
        out_shape=pltpu.VMEM(tokens.shape, tokens.dtype),
        in_specs=[anywhere] + [vmem] * 4 + [anywhere] * 4,
        out_specs=vmem,
        scratch_shapes=[
            pltpu.VMEM((capacity, width), bf16),
            pltpu.VMEM((4, section_count, capacity, width), bf16),
            pltpu.VMEM((4, slots, BLOCK), f32),
            pltpu.VMEM((host_rows, depth), bf16),
            pltpu.VMEM((seq_count, w_key.shape[0], kv_cols), bf16),
            pltpu.VMEM((heads_half, seq_count, w_query.shape[0], HEAD_DIM), bf16),
            pltpu.VMEM((parts_o, seq_count, w_out.shape[0], part_o), bf16),
            pltpu.VMEM((2, seq_count * capacity, kv_cols), bf16),
            pltpu.VMEM((heads_half, host_rows, HEAD_DIM), bf16),
            pltpu.VMEM((heads_half, host_rows, HEAD_DIM), f32),
            pltpu.VMEM((heads_half, host_rows, 1), f32),
            pltpu.VMEM((2, heads_half, section_count, host_rows, HEAD_DIM), bf16),
            pltpu.VMEM((4, parts_o, capacity, part_o), bf16),
            pltpu.VMEM((2, parts_o, capacity, part_o), bf16),
            pltpu.VMEM((line // tile_spots, tile), jnp.int32),
            dma((1,)),
            dma((chunk_count,)),
            dma((chunk_count,)),
            dma((1,)),
            dma((2, 2)),
            dma((2, section_count * 2 + 1)),
            dma((1,)),
            dma((2,)),
            dma((2, line - 2)),
            dma((line,)),
            dma((2, line)),
            dma((heads_half, 2)),
            dma((heads_half, section_count * 2 + 1)),
            dma((1,)),
            dma((parts_o,)),
        ],
        compiler_params=pltpu.CompilerParams(collective_id=0, has_side_effects=True),
    )(
        tokens,
        norm_gain[None, :],
        router_gate.reshape(tok_rows // BLOCK, BLOCK),
        blocks[None, :],
        block_counts[None, :],
        w_query,
        w_key,
        w_value,
        w_out,
    )


def solution(mesh):
    return jax.shard_map(
        local,
        mesh=mesh,
        in_specs=(
            P("seq", "section"),
            P(),
            P("seq", "section"),
            P("seq", "section"),
            P("seq", "section"),
            P("seq", "section"),
            P("seq"),
            P(),
            P(),
        ),
        out_specs=P("seq", "section"),
        check_vma=False,
    )
```

time: 52.8 us -> 42.2 us (0.80)
  Pallas kernels: 52.5 us -> 41.2 us
  local copies, waits for them, and re-layouts: 0 us -> 0.8 us
    pallas_call x1, Pallas kernels: 50.6 us -> 41.2 us  [local(): pl.pallas_call(functools.partial(kernel, seq_count, section_count, tile_s...]
    pallas_call x1 -> x0, Pallas kernels: 1.91 us -> none  [local(): pl.pallas_call(put, out_shape=jax.ShapeDtypeStruct(tokens.shape, tokens.d...]
    unnamed x0 -> x1, local copies, waits for them, and re-layouts: none -> 0.8 us
where the time goes in v3:
time: 42.2 us; the launch traced here: 42 us
  Pallas kernels  41.2 us (98%)
  local copies, waits for them, and re-layouts  0.8 us (2%)
    pallas_call x1, Pallas kernels, local(): pl.pallas_call(functools.partial(kernel, seq_count, section_count, tile_s...  41.2 us

profile of v3, /device:TPU:25, one launch (start us, length us, event | category | flops | bytes accessed | tf_op | source)
XLA Modules:
  0.0 42.0 jit_solution(18177511599488935759)
XLA Ops:
  0.0 41.2 %shard_map.91 = bf16[512,512]{1,0:T(8,128)(2,1)S(1)} custom-call(bf16[512,512]{1,0:T(8,128)(2,1)} %tokens_hbm.1, f32[1,2048]{1,0:T(1,128)} %bitcast.4, f32[4,128]{1,0:T(4,128)} %bitcast.5, s32[1,8]{1,0:T(1,128)} %bitcast.6, s32[1,8]{1,0:T(1,128)} %bitcast.7, bf16[256,512]{1,0:T(8,128)(2,1)} %wq_in.1, bf16[256,128]{1,0:T(8,128)(2,1)} %wk_in.1, ...), custom_call_target="tpu_custom_call" | custom-call | tf_op jit(solution)/shard_map/pallas_call | solution.py:661
  41.2 0.8 %copy.11 = bf16[512,512]{1,0:T(8,128)(2,1)} copy(bf16[512,512]{1,0:T(8,128)(2,1)S(1)} %shard_map.91) | data formatting | bytes 1048576

commit v4 on v3

--- a/solution.py
+++ b/solution.py
@@ -42,15 +42,19 @@
     section_count,
     tile_spots,
     tokens_hbm,
-    gain_ref,
-    gate_ref,
-    chosen_ref,
-    count_ref,
+    gain_hbm,
+    gate_hbm,
+    chosen_hbm,
+    count_hbm,
     wq_in,
     wk_in,
     wv_in,
     wo_in,
     mixed_ref,
+    gain_ref,
+    gate_ref,
+    chosen_ref,
+    count_ref,
     out_ref,
     rows_all,
     gate_rows,
@@ -66,7 +70,7 @@
     results,
     returned,
     key_slots,
-    tokens_sem,
+    load_sems,
     weight_send,
     weight_recv,
     guest_send,
@@ -333,8 +337,20 @@
         )
 
     barrier = pltpu.get_barrier_semaphore()
-    load_tokens = pltpu.make_async_copy(tokens_hbm, mixed_ref, tokens_sem.at[0])
-    load_tokens.start()
+    loads = [
+        pltpu.make_async_copy(source, target, load_sems.at[number])
+        for number, (source, target) in enumerate(
+            (
+                (tokens_hbm, mixed_ref),
+                (chosen_hbm, chosen_ref),
+                (gate_hbm, gate_ref),
+                (gain_hbm, gain_ref),
+                (count_hbm, count_ref),
+            )
+        )
+    ]
+    for load in loads:
+        load.start()
 
     def greet(other):
         @pl.when((other != me) & (active | (other >= first * 2) & (other < (last + 1) * 2)))
@@ -353,7 +369,8 @@
         lane = lax.broadcasted_iota(jnp.int32, row.shape, 1)
         return jnp.sum(jnp.where(lane == index, row, 0), axis=1, keepdims=True)
 
-    load_tokens.wait()
+    for load in loads:
+        load.wait()
     for slot in range(slots):
         number = pick(chosen_ref, me * slots + slot)
         rows = mixed_ref[:BLOCK, :]
@@ -661,9 +678,13 @@
     return pl.pallas_call(
         functools.partial(kernel, seq_count, section_count, tile_spots),
         out_shape=pltpu.VMEM(tokens.shape, tokens.dtype),
-        in_specs=[anywhere] + [vmem] * 4 + [anywhere] * 4,
+        in_specs=[anywhere] * 9,
         out_specs=vmem,
         scratch_shapes=[
+            pltpu.VMEM((1, depth), f32),
+            pltpu.VMEM((tok_rows // BLOCK, BLOCK), f32),
+            pltpu.VMEM((1, blocks.shape[0]), jnp.int32),
+            pltpu.VMEM((1, seq_count), jnp.int32),
             pltpu.VMEM((capacity, width), bf16),
             pltpu.VMEM((4, section_count, capacity, width), bf16),
             pltpu.VMEM((4, slots, BLOCK), f32),
@@ -679,7 +700,7 @@
             pltpu.VMEM((4, parts_o, capacity, part_o), bf16),
             pltpu.VMEM((2, parts_o, capacity, part_o), bf16),
             pltpu.VMEM((line // tile_spots, tile), jnp.int32),
-            dma((1,)),
+            dma((5,)),
             dma((chunk_count,)),
             dma((chunk_count,)),
             dma((1,)),

time: 42.2 us -> 41.5 us (0.983)
  Pallas kernels: 41.2 us -> 40.5 us
    pallas_call x1, Pallas kernels: 41.2 us -> 40.5 us  [local(): pl.pallas_call(functools.partial(kernel, seq_count, section_count, tile_s...]
where the time goes in v4:
time: 41.5 us; the launch traced here: 41.4 us
  Pallas kernels  40.5 us (98%)
  local copies, waits for them, and re-layouts  0.8 us (2%)
    pallas_call x1, Pallas kernels, local(): pl.pallas_call(functools.partial(kernel, seq_count, section_count, tile_s...  40.5 us

profile of v4, /device:TPU:25, one launch (start us, length us, event | category | flops | bytes accessed | tf_op | source)
XLA Modules:
  0.0 41.4 jit_solution(13935256694410596074)
XLA Ops:
  0.0 40.5 %shard_map.91 = bf16[512,512]{1,0:T(8,128)(2,1)S(1)} custom-call(bf16[512,512]{1,0:T(8,128)(2,1)} %tokens_hbm.1, f32[1,2048]{1,0:T(1,128)} %bitcast.4, f32[4,128]{1,0:T(4,128)} %bitcast.5, s32[1,8]{1,0:T(1,128)} %bitcast.6, s32[1,8]{1,0:T(1,128)} %bitcast.7, bf16[256,512]{1,0:T(8,128)(2,1)} %wq_in.1, bf16[256,128]{1,0:T(8,128)(2,1)} %wk_in.1, ...), custom_call_target="tpu_custom_call" | custom-call | tf_op jit(solution)/shard_map/pallas_call | solution.py:678
  40.6 0.8 %copy.11 = bf16[512,512]{1,0:T(8,128)(2,1)} copy(bf16[512,512]{1,0:T(8,128)(2,1)S(1)} %shard_map.91) | data formatting | bytes 1048576

commit v5 on v4

--- a/solution.py
+++ b/solution.py
@@ -598,6 +598,7 @@
         for part in range(parts_o):
             receive_weight((OUT, part))
             pl.when(has_guest)(lambda: finish(1, part))
+        for part in range(parts_o):
             finish(0, part)
 
         rows_gather(0).drain()

time: 41.5 us -> 41.2 us (level)
  no operation moved by 1% of the time
where the time goes in v5:
time: 41.2 us; the launch traced here: 41 us
  Pallas kernels  40.2 us (98%)
  local copies, waits for them, and re-layouts  0.8 us (2%)
    pallas_call x1, Pallas kernels, local(): pl.pallas_call(functools.partial(kernel, seq_count, section_count, tile_s...  40.2 us

profile of v5, /device:TPU:25, one launch (start us, length us, event | category | flops | bytes accessed | tf_op | source)
XLA Modules:
  0.0 41.0 jit_solution(275307514322514037)
XLA Ops:
  0.0 40.2 %shard_map.91 = bf16[512,512]{1,0:T(8,128)(2,1)S(1)} custom-call(bf16[512,512]{1,0:T(8,128)(2,1)} %tokens_hbm.1, f32[1,2048]{1,0:T(1,128)} %bitcast.4, f32[4,128]{1,0:T(4,128)} %bitcast.5, s32[1,8]{1,0:T(1,128)} %bitcast.6, s32[1,8]{1,0:T(1,128)} %bitcast.7, bf16[256,512]{1,0:T(8,128)(2,1)} %wq_in.1, bf16[256,128]{1,0:T(8,128)(2,1)} %wk_in.1, ...), custom_call_target="tpu_custom_call" | custom-call | tf_op jit(solution)/shard_map/pallas_call | solution.py:679
  40.2 0.8 %copy.11 = bf16[512,512]{1,0:T(8,128)(2,1)} copy(bf16[512,512]{1,0:T(8,128)(2,1)S(1)} %shard_map.91) | data formatting | bytes 1048576

commit v6 on v5

--- a/solution.py
+++ b/solution.py
@@ -398,6 +398,17 @@
         for chunk in chunks:
             send_weight(chunk)
 
+    def settle_cols(cols):
+        for slot in range(slots):
+            number = pick(chosen_ref, me * slots + slot)
+            number = jnp.where(pick(count_ref, me) > slot, number, gate_ref.shape[0])
+            fresh = out_ref[slot * BLOCK : (slot + 1) * BLOCK, cols]
+            for block in range(gate_ref.shape[0]):
+                rows = pl.ds(block * BLOCK, BLOCK)
+                mixed_ref[rows, cols] = jnp.where(
+                    jnp.broadcast_to(number, fresh.shape) == block, fresh, mixed_ref[rows, cols]
+                )
+
     def gate_column(place):
         wide = gate_rows[place]
         square = lax.broadcasted_iota(jnp.int32, (BLOCK, BLOCK), 0) == lax.broadcasted_iota(
@@ -624,8 +635,11 @@
             finish_weight(chunk, hosts * 2 - 1)
         for part in range(parts_o):
             cols = pl.ds(pl.multiple_of((1 - core) * half_o + part * part_o, part_o), part_o)
+            own = pl.ds(pl.multiple_of(core * half_o + part * part_o, part_o), part_o)
+            settle_cols(own)
             await_bytes(returned.at[1 - core, part], back_recv.at[part])
             out_ref[:, cols] = returned[1 - core, part]
+            settle_cols(cols)
 
     @pl.when(jnp.logical_not(active))
     def _():
@@ -638,17 +652,7 @@
             for half in range(2):
                 cols = pl.ds(half * half_o + part * part_o, part_o)
                 out_ref[:, cols] = returned[half, part]
-
-    for slot in range(slots):
-        number = pick(chosen_ref, me * slots + slot)
-        count = pick(count_ref, me)
-        number = jnp.where(count > slot, number, gate_ref.shape[0])
-        fresh = out_ref[slot * BLOCK : (slot + 1) * BLOCK, :]
-        for block in range(gate_ref.shape[0]):
-            rows = pl.ds(block * BLOCK, BLOCK)
-            mixed_ref[rows, :] = jnp.where(
-                jnp.broadcast_to(number, fresh.shape) == block, fresh, mixed_ref[rows, :]
-            )
+                settle_cols(cols)
 
 
 def local(

time: 41.2 us -> 41.4 us (level)
  no operation moved by 1% of the time
where the time goes in v6:
time: 41.4 us; the launch traced here: 41 us
  Pallas kernels  40.2 us (97%)
  local copies, waits for them, and re-layouts  0.8 us (2%)
    pallas_call x1, Pallas kernels, local(): pl.pallas_call(functools.partial(kernel, seq_count, section_count, tile_s...  40.2 us

profile of v6, /device:TPU:25, one launch (start us, length us, event | category | flops | bytes accessed | tf_op | source)
XLA Modules:
  0.0 41.0 jit_solution(12136664655361077787)
XLA Ops:
  0.0 40.2 %shard_map.91 = bf16[512,512]{1,0:T(8,128)(2,1)S(1)} custom-call(bf16[512,512]{1,0:T(8,128)(2,1)} %tokens_hbm.1, f32[1,2048]{1,0:T(1,128)} %bitcast.4, f32[4,128]{1,0:T(4,128)} %bitcast.5, s32[1,8]{1,0:T(1,128)} %bitcast.6, s32[1,8]{1,0:T(1,128)} %bitcast.7, bf16[256,512]{1,0:T(8,128)(2,1)} %wq_in.1, bf16[256,128]{1,0:T(8,128)(2,1)} %wk_in.1, ...), custom_call_target="tpu_custom_call" | custom-call | tf_op jit(solution)/shard_map/pallas_call | solution.py:683
  40.2 0.8 %copy.11 = bf16[512,512]{1,0:T(8,128)(2,1)} copy(bf16[512,512]{1,0:T(8,128)(2,1)S(1)} %shard_map.91) | data formatting | bytes 1048576
